TPU v7x, 1024 devices: a whole 4x8x16 slice. The times are simulated.
1024 devices in a mesh: outer: 8 (over x, core), inner: 128 (over z, y).
Axes of the slice: x: 4, y: 8, z: 16, core: 2. Of those that a mesh axis runs over, the one named last changes fastest.
Arguments:
- leaf_q: float32 [262144, 128], P(('outer', 'inner')), may hold values from -0.375 to 0.375
- q_cot: float32 [262144, 128], P(('outer', 'inner')), may hold values from -6 to 6
- leaf_tri: float32 [131072, 128], P(('outer', 'inner')), as said below
- node_blocks: bfloat16 [5, 131072, 128], P(None, ('outer', 'inner')), as said below
- node_tri: bfloat16 [5, 131072, 128], P(None, ('outer', 'inner')), as said below
- root_cot: float32 [128, 128], replicated, may hold values from -6 to 6
Outputs:
- mat_grad: float32 [262144, 128], P(('outer', 'inner'))
Inputs may be any that keep to these rules, and one draw needn't show every extreme that they name: `leaf_tri`: upper triangular; diagonal between 1 and 3. `node_blocks`: at each level, every leaf holds the block of its own child subtree, and all leaves of one child subtree hold equal blocks. `node_tri`: upper triangular with diagonal between 1 and 3; at each level all leaves of one node hold equal triangles.
All inputs are finite; a program needn't handle non-finite values.
Results may differ from a plain program's by a relative error of at most 0.0003.
Values sent between devices are 32-bit elements; how exact they have to be, the bound alone decides.
No kernel may reach another device: no remote copies, remote signals or barrier semaphores. Data moves between devices by JAX's collectives and lax.ppermute only.
A program may use at most 32 MiB of HBM per device.

v0:
```python
import jax
import jax.numpy as jnp
from jax import lax
from jax.sharding import PartitionSpec as P

BLOCK = 32


def partner(value, axis, stride):
    mask = 2**stride
    pairs = [(source, source ^ mask) for source in range(lax.axis_size(axis))]
    return lax.ppermute(value, axis, pairs)


def matmul(left_side, right_side):
    return jnp.dot(
        left_side, right_side, precision=lax.Precision.HIGHEST, preferred_element_type=jnp.float32
    )


def inner_product(left_side, right_side):
    return lax.dot_general(
        left_side,
        right_side,
        (((0,), (0,)), ((), ())),
        precision=lax.Precision.HIGHEST,
        preferred_element_type=jnp.float32,
    )


def mirror_lower(matrix):
    return jnp.tril(matrix) + jnp.tril(matrix, -1).T


def small_inverse(block):
    order = block.shape[-1]
    diag_vals = jnp.diagonal(block)
    eye_small = jnp.eye(order, dtype=jnp.float32)
    nilpotent = -jnp.triu(block, 1) / diag_vals[:, None]
    product = eye_small + nilpotent
    power = 2
    while power < order:
        nilpotent = matmul(nilpotent, nilpotent)
        product = matmul(product, eye_small + nilpotent)
        power = power * 2
    return product / diag_vals[None, :]


def tri_inverse(triangle):
    order = triangle.shape[-1]
    count = order // BLOCK
    inverses = [
        small_inverse(triangle[k * BLOCK : (k + 1) * BLOCK, k * BLOCK : (k + 1) * BLOCK])
        for k in range(count)
    ]
    span = BLOCK
    while len(inverses) > 1:
        joined = []
        for pair in range(len(inverses) // 2):
            start = pair * 2 * span
            upper_inv = inverses[2 * pair]
            lower_inv = inverses[2 * pair + 1]
            corner = triangle[start : start + span, start + span : start + 2 * span]
            linked = -matmul(matmul(upper_inv, corner), lower_inv)
            top_rows = jnp.concatenate([upper_inv, linked], axis=1)
            bottom_rows = jnp.concatenate([jnp.zeros_like(lower_inv), lower_inv], axis=1)
            joined.append(jnp.concatenate([top_rows, bottom_rows], axis=0))
        inverses = joined
        span = span * 2
    return inverses[0]


def right_solve(triangle, values):
    return matmul(values, tri_inverse(triangle).T)


def bit_groups(bit_count):
    groups = []
    first_bit = 0
    while first_bit < bit_count:
        span_bits = min(2, bit_count - first_bit)
        groups.append((first_bit, span_bits))
        first_bit = first_bit + span_bits
    return groups


def on_device(leaf_q, q_cot, leaf_tri, node_blocks, node_tri, root_cot):
    bit_count = lax.axis_size("inner").bit_length() - 1
    groups = bit_groups(bit_count)
    levels_count = len(groups) + 1
    blocks_all = node_blocks.astype(jnp.float32)
    tris_all = node_tri.astype(jnp.float32)
    leaf_sums = inner_product(leaf_q, q_cot)
    child_sums = [leaf_sums]
    current = leaf_sums
    for height in range(levels_count - 1):
        first_bit, span_bits = groups[height]
        current = inner_product(blocks_all[height], current)
        for bit_index in range(first_bit, first_bit + span_bits):
            current = current + partner(current, "inner", bit_index)
        child_sums.append(current)
    top_part = inner_product(blocks_all[levels_count - 1], current)
    top_sum = lax.psum(top_part, "outer")
    upper_path = None
    cot_tri = root_cot
    for height in reversed(range(levels_count)):
        node_sum = top_sum if height == levels_count - 1 else child_sums[height + 1]
        own_sum = child_sums[height]
        own_block = blocks_all[height]
        node_triangle = tris_all[height]
        if upper_path is None:
            middle = matmul(node_triangle, cot_tri.T) - node_sum.T
            right_side = own_sum + matmul(own_block, mirror_lower(middle))
            upper_path = own_block
        else:
            middle = matmul(node_triangle, cot_tri.T) - matmul(upper_path, node_sum.T)
            right_side = matmul(own_sum, upper_path.T) + matmul(own_block, mirror_lower(middle))
            upper_path = matmul(own_block, upper_path)
        cot_tri = right_solve(node_triangle, right_side)
    leaf_cot = matmul(q_cot, upper_path.T)
    middle = matmul(leaf_tri, cot_tri.T) - matmul(upper_path, leaf_sums.T)
    return right_solve(leaf_tri, leaf_cot + matmul(leaf_q, mirror_lower(middle)))


def solution(mesh):
    return jax.shard_map(
        on_device,
        mesh=mesh,
        in_specs=(
            P(("outer", "inner"), None),
            P(("outer", "inner"), None),
            P(("outer", "inner"), None),
            P(None, ("outer", "inner"), None),
            P(None, ("outer", "inner"), None),
            P(),
        ),
        out_specs=P(("outer", "inner"), None),
        check_vma=False,
    )
```

profile of v0, /device:TPU:1, one launch (start us, length us, event | category | flops | bytes accessed | tf_op | source)
XLA Modules:
  0.0 260.2 jit_solution(10781374842546847806)
XLA Ops:
  7.4 1.3 fusion.410
  9.0 4.0 %collective-permute-start = (f32[128,128]{0,1:T(8,128)S(1)}, f32[128,128]{0,1:T(8,128)S(1)}, u32[]{:S(2)}, u32[]{:S(2)}) collective-permute-start(f32[128,128]{0,1:T(8,128)S(1)} %convolution_bitcast_fusion.9), channel_id=1, source_target_pairs={{0,1},{1,0},{2,3},{3,2},{4,5},{5,4},{6,7},{7,6},{8,9},{9,8},{10,11... | collective-permute-start | bytes 196616 | tf_op jit(solution)/shard_map/ppermute | solution.py:12
  15.8 1.0 fusion.331
  18.6 1.0 fusion.332
  21.4 1.0 fusion.333
  27.1 1.0 fusion.327
  29.9 1.0 fusion.328
  38.5 1.0 fusion.323
  41.3 1.0 fusion.324
  52.6 1.0 fusion.320
  96.6 4.2 %collective-permute-start.1 = (f32[128,128]{0,1:T(8,128)S(1)}, f32[128,128]{0,1:T(8,128)S(1)}, u32[]{:S(2)}, u32[]{:S(2)}) collective-permute-start(f32[128,128]{0,1:T(8,128)S(1)} %add.535), channel_id=1, source_target_pairs={{0,2},{1,3},{2,0},{3,1},{4,6},{5,7},{6,4},{7,5},{8,10},{9,11},{10,... | collective-permute-start | bytes 196616 | tf_op jit(solution)/shard_map/ppermute | solution.py:12
  100.9 2.1 collective-permute-done.1
  103.2 6.0 %collective-permute-start.2 = (f32[128,128]{0,1:T(8,128)S(1)}, f32[128,128]{0,1:T(8,128)S(1)}, u32[]{:S(2)}, u32[]{:S(2)}) collective-permute-start(f32[128,128]{0,1:T(8,128)S(1)} %convolution_bitcast_fusion.8), channel_id=1, source_target_pairs={{0,4},{1,5},{2,6},{3,7},{4,0},{5,1},{6,2},{7,3},{8,12},{9,13},{10,... | collective-permute-start | bytes 196616 | tf_op jit(solution)/shard_map/ppermute | solution.py:12
  109.3 2.9 %collective-permute-done.2 = f32[128,128]{0,1:T(8,128)S(1)} collective-permute-done((f32[128,128]{0,1:T(8,128)S(1)}, f32[128,128]{0,1:T(8,128)S(1)}, u32[]{:S(2)}, u32[]{:S(2)}) %collective-permute-start.2) | collective-permute-done | bytes 65568 | tf_op jit(solution)/shard_map/ppermute | solution.py:12
  112.2 4.0 %collective-permute-start.3 = (f32[128,128]{0,1:T(8,128)S(1)}, f32[128,128]{0,1:T(8,128)S(1)}, u32[]{:S(2)}, u32[]{:S(2)}) collective-permute-start(f32[128,128]{0,1:T(8,128)S(1)} %add.537), channel_id=1, source_target_pairs={{0,8},{1,9},{2,10},{3,11},{4,12},{5,13},{6,14},{7,15},{8,0},{9,1},... | collective-permute-start | bytes 196616 | tf_op jit(solution)/shard_map/ppermute | solution.py:12
  116.7 1.3 collective-permute-done.3
  118.1 5.8 %collective-permute-start.4 = (f32[128,128]{0,1:T(8,128)S(1)}, f32[128,128]{0,1:T(8,128)S(1)}, u32[]{:S(2)}, u32[]{:S(2)}) collective-permute-start(f32[128,128]{0,1:T(8,128)S(1)} %convolution_bitcast_fusion.7), channel_id=1, source_target_pairs={{0,16},{1,17},{2,18},{3,19},{4,20},{5,21},{6,22},{7,23},{8,24},{9,... | collective-permute-start | bytes 196616 | tf_op jit(solution)/shard_map/ppermute | solution.py:12
  123.9 1.6 collective-permute-done.4
  125.6 10.6 %collective-permute-start.5 = (f32[128,128]{0,1:T(8,128)S(1)}, f32[128,128]{0,1:T(8,128)S(1)}, u32[]{:S(2)}, u32[]{:S(2)}) collective-permute-start(f32[128,128]{0,1:T(8,128)S(1)} %add.539), channel_id=1, source_target_pairs={{0,32},{1,33},{2,34},{3,35},{4,36},{5,37},{6,38},{7,39},{8,40},{9,... | collective-permute-start | bytes 196616 | tf_op jit(solution)/shard_map/ppermute | solution.py:12
  136.6 1.3 collective-permute-done.5
  138.1 13.5 %collective-permute-start.6 = (f32[128,128]{0,1:T(8,128)S(1)}, f32[128,128]{0,1:T(8,128)S(1)}, u32[]{:S(2)}, u32[]{:S(2)}) collective-permute-start(f32[128,128]{0,1:T(8,128)S(1)} %convolution_bitcast_fusion.6), channel_id=1, source_target_pairs={{0,64},{1,65},{2,66},{3,67},{4,68},{5,69},{6,70},{7,71},{8,72},{9,... | collective-permute-start | bytes 196616 | tf_op jit(solution)/shard_map/ppermute | solution.py:12
  152.0 2.0 collective-permute-done.6
  155.1 89.3 %all-reduce.20.cloned.1.call-done = f32[128,128]{1,0:T(8,128)} async-done(((f32[128,128]{1,0:T(8,128)}), f32[128,128]{1,0:T(8,128)}) %all-reduce.20.cloned.1.call-update) | async-done | bytes 65552 | tf_op jit(solution)/shard_map/psum | solution.py:103
  252.2 1.1 fusion.2
  (341 shorter events, 86.0 us)
Async XLA Ops:
  6.5 0.9 copy-start
  6.5 2.2 copy-start.1
  6.5 238.0 %all-reduce.20.cloned.1.call-start = ((), (), s32[]{:S(2)}) async-start(), calls=%async_computation | async-start | bytes 131072 | tf_op jit(solution)/shard_map/psum | solution.py:103
  8.7 4.3 %copy-start.2 = (bf16[5,128,128]{2,1,0:T(8,128)(2,1)S(1)}, bf16[5,128,128]{2,1,0:T(8,128)(2,1)}, u32[]{:S(2)}) copy-start(bf16[5,128,128]{2,1,0:T(8,128)(2,1)} %param.10) | copy-start | bytes 491524
  9.0 87.5 %collective-permute-start = (f32[128,128]{0,1:T(8,128)S(1)}, f32[128,128]{0,1:T(8,128)S(1)}, u32[]{:S(2)}, u32[]{:S(2)}) collective-permute-start(f32[128,128]{0,1:T(8,128)S(1)} %convolution_bitcast_fusion.9), channel_id=1, source_target_pairs={{0,1},{1,0},{2,3},{3,2},{4,5},{5,4},{6,7},{7,6},{8,9},{9,8},{10,11... | collective-permute-start | bytes 196616 | tf_op jit(solution)/shard_map/ppermute | solution.py:12
  13.1 0.6 copy-start.7
  13.1 1.5 copy-start.8
  13.1 21.7 %copy-start.5 = (f32[128,128]{1,0:T(8,128)}, f32[128,128]{1,0:T(8,128)S(1)}, u32[]{:S(2)}) copy-start(f32[128,128]{1,0:T(8,128)S(1)} %get-tuple-element.8) | copy-start | bytes 196612
  13.2 21.7 %copy-start.6 = (f32[128,128]{1,0:T(8,128)}, f32[128,128]{1,0:T(8,128)S(1)}, u32[]{:S(2)}) copy-start(f32[128,128]{1,0:T(8,128)S(1)} %get-tuple-element.7) | copy-start | bytes 196612
  64.2 0.8 copy-start.3
  89.6 0.8 copy-start.10
  96.6 6.5 %collective-permute-start.1 = (f32[128,128]{0,1:T(8,128)S(1)}, f32[128,128]{0,1:T(8,128)S(1)}, u32[]{:S(2)}, u32[]{:S(2)}) collective-permute-start(f32[128,128]{0,1:T(8,128)S(1)} %add.535), channel_id=1, source_target_pairs={{0,2},{1,3},{2,0},{3,1},{4,6},{5,7},{6,4},{7,5},{8,10},{9,11},{10,... | collective-permute-start | bytes 196616 | tf_op jit(solution)/shard_map/ppermute | solution.py:12
  103.2 9.0 %collective-permute-start.2 = (f32[128,128]{0,1:T(8,128)S(1)}, f32[128,128]{0,1:T(8,128)S(1)}, u32[]{:S(2)}, u32[]{:S(2)}) collective-permute-start(f32[128,128]{0,1:T(8,128)S(1)} %convolution_bitcast_fusion.8), channel_id=1, source_target_pairs={{0,4},{1,5},{2,6},{3,7},{4,0},{5,1},{6,2},{7,3},{8,12},{9,13},{10,... | collective-permute-start | bytes 196616 | tf_op jit(solution)/shard_map/ppermute | solution.py:12
  112.2 5.7 %collective-permute-start.3 = (f32[128,128]{0,1:T(8,128)S(1)}, f32[128,128]{0,1:T(8,128)S(1)}, u32[]{:S(2)}, u32[]{:S(2)}) collective-permute-start(f32[128,128]{0,1:T(8,128)S(1)} %add.537), channel_id=1, source_target_pairs={{0,8},{1,9},{2,10},{3,11},{4,12},{5,13},{6,14},{7,15},{8,0},{9,1},... | collective-permute-start | bytes 196616 | tf_op jit(solution)/shard_map/ppermute | solution.py:12
  118.1 7.5 %collective-permute-start.4 = (f32[128,128]{0,1:T(8,128)S(1)}, f32[128,128]{0,1:T(8,128)S(1)}, u32[]{:S(2)}, u32[]{:S(2)}) collective-permute-start(f32[128,128]{0,1:T(8,128)S(1)} %convolution_bitcast_fusion.7), channel_id=1, source_target_pairs={{0,16},{1,17},{2,18},{3,19},{4,20},{5,21},{6,22},{7,23},{8,24},{9,... | collective-permute-start | bytes 196616 | tf_op jit(solution)/shard_map/ppermute | solution.py:12
  125.6 12.3 %collective-permute-start.5 = (f32[128,128]{0,1:T(8,128)S(1)}, f32[128,128]{0,1:T(8,128)S(1)}, u32[]{:S(2)}, u32[]{:S(2)}) collective-permute-start(f32[128,128]{0,1:T(8,128)S(1)} %add.539), channel_id=1, source_target_pairs={{0,32},{1,33},{2,34},{3,35},{4,36},{5,37},{6,38},{7,39},{8,40},{9,... | collective-permute-start | bytes 196616 | tf_op jit(solution)/shard_map/ppermute | solution.py:12
  138.1 15.8 %collective-permute-start.6 = (f32[128,128]{0,1:T(8,128)S(1)}, f32[128,128]{0,1:T(8,128)S(1)}, u32[]{:S(2)}, u32[]{:S(2)}) collective-permute-start(f32[128,128]{0,1:T(8,128)S(1)} %convolution_bitcast_fusion.6), channel_id=1, source_target_pairs={{0,64},{1,65},{2,66},{3,67},{4,68},{5,69},{6,70},{7,71},{8,72},{9,... | collective-permute-start | bytes 196616 | tf_op jit(solution)/shard_map/ppermute | solution.py:12
  244.5 1.0 copy-start.9
  251.0 0.9 copy-start.4
Sparse Core Ops, SparseCore 0:
  155.0 89.4 all-reduce.19
where the time goes:
time: 265 us; the launch traced here: 260 us
  waiting for transfers between devices  101 us (38%)
  matrix products  72.3 us (27%)
  starting transfers between devices  48.2 us (18%)
  local copies, waits for them, and re-layouts  23.5 us (9%)
  between operations  15.1 us (6%)
    psum x1, waiting for transfers between devices, on_device(): top_sum = lax.psum(top_part, 'outer')  89.3 us
    dot_general x260, matrix products, matmul(): jnp.dot(left_side, right_side, precision=lax.Precision.HIGHEST, preferred...  69.4 us
    ppermute x7, starting transfers between devices, partner(): return lax.ppermute(value, axis, pairs)  48.2 us
    gather x24, local copies, waits for them, and re-layouts, small_inverse(): diag_vals = jnp.diagonal(block)  17.6 us
    ppermute x7, waiting for transfers between devices, partner(): return lax.ppermute(value, axis, pairs)  11.2 us
  transfers between devices with their start and end apart: 8, of which 7 were waited for; matrix products, arithmetic and copies ran while one was open for 32% of the time, Pallas kernels for 0%

commit v1 on v0

v1 whole, which is shorter than its diff:
```python
import jax
import jax.numpy as jnp
from jax import lax
from jax.experimental import pallas as pl
from jax.experimental.pallas import tpu as pltpu
from jax.sharding import Mesh, PartitionSpec as P

N = 128
BLOCK = 32
PIECE = 16
ROWS = 256
LEVELS = 5
N_Y = 8
N_Z = 16
N_OUTER = 8

F32 = jnp.float32
BF16 = jnp.bfloat16


def split3(value):
    high = value.astype(BF16)
    rest = value - high.astype(F32)
    middle = rest.astype(BF16)
    low = (rest - middle.astype(F32)).astype(BF16)
    return high, middle, low


def dot(left, right, dims):
    return lax.dot_general(left, right, (dims, ((), ())), preferred_element_type=F32)


NN = ((1,), (0,))
NT = ((1,), (1,))


def mm(left, right, dims=NN):
    rows = left.shape[0]
    lh, lm, ll = split3(left)
    rh, rm, rl = split3(right)
    first = dot(jnp.concatenate([lh, lm, ll], axis=0), rh, dims)
    second = dot(jnp.concatenate([lh, lm], axis=0), rm, dims)
    third = dot(lh, rl, dims)
    small = first[2 * rows :] + second[rows:] + third
    return first[:rows] + (first[rows : 2 * rows] + second[:rows] + small)


def mm_exact(left, right, dims=NN):
    rows = left.shape[0]
    lh, lm, ll = split3(left)
    full = dot(jnp.concatenate([lh, lm, ll], axis=0), right, dims)
    return full[:rows] + (full[rows : 2 * rows] + full[2 * rows :])


def iotas(rows=N):
    return (
        lax.broadcasted_iota(jnp.int32, (rows, N), 0),
        lax.broadcasted_iota(jnp.int32, (rows, N), 1),
    )


def mirror_lower(matrix):
    row, col = iotas()
    return jnp.where(row >= col, matrix, matrix.T)


def tri_inverse(triangle):
    row, col = iotas()
    on_diag = row == col
    diag_col = jnp.sum(jnp.where(on_diag, triangle, 0.0), axis=1, keepdims=True)
    diag_row = jnp.sum(jnp.where(on_diag, triangle, 0.0), axis=0, keepdims=True)
    same = (row // BLOCK) == (col // BLOCK)
    strict = jnp.where(same & (row < col), -triangle, 0.0) / diag_col

    def packed(matrix):
        return (matrix[0:32] + matrix[32:64]) + (matrix[64:96] + matrix[96:128])

    def spread(rows):
        return jnp.where(same, jnp.concatenate([rows] * 4, axis=0), 0.0)

    small_row, small_col = iotas(BLOCK)
    eye = jnp.where(small_row == small_col % BLOCK, 1.0, 0.0).astype(F32)
    power = packed(strict)
    product = eye + power
    power = mm(power, strict)
    for _ in range(3):
        both = mm(jnp.concatenate([power, product], axis=0), spread(power))
        product = product + both[BLOCK:]
        power = both[:BLOCK]
    product = product + mm(product, spread(power))
    inverse = product / diag_row
    block_inverse = spread(inverse)
    corner = jnp.where((row // 64 == col // 64) & (row // 32 < col // 32), triangle, 0.0)
    linked = mm(mm(inverse, corner), block_inverse)
    odd = (small_col // BLOCK) % 2 == 1
    top = jnp.where(odd, -linked, inverse)
    bottom = jnp.where(odd, inverse, 0.0)
    pair = jnp.concatenate([top, bottom], axis=0)
    pair_inverse = jnp.where(row // 64 == col // 64, jnp.concatenate([pair, pair], axis=0), 0.0)
    corner = jnp.where(row // 64 < col // 64, triangle, 0.0)
    linked = mm(mm(pair, corner), pair_inverse)
    upper = pair_inverse[:64] - linked
    return jnp.concatenate([upper, pair_inverse[64:]], axis=0)


def leaf_values(leaf_q, q_cot, block_1, block_2):
    sums_t = mm(q_cot.T, leaf_q)
    first_t = mm_exact(sums_t, block_1)
    second_t = mm_exact(first_t, block_2)
    return sums_t, first_t, second_t


def leaf_kernel(q_ref, g_ref, blocks_ref, sums_ref, send_ref):
    sums_t, first_t, second_t = leaf_values(q_ref[...], g_ref[...], blocks_ref[0], blocks_ref[1])
    sums_ref[...] = sums_t
    for y in range(N_Y):
        send_ref[y, 0:PIECE] = first_t[y * PIECE : (y + 1) * PIECE]
        send_ref[y, PIECE : 2 * PIECE] = second_t[y * PIECE : (y + 1) * PIECE]


def near_kernel(z_ref, recv_ref, blocks_ref, kept_ref, send_ref):
    z = z_ref[0]
    halves = [sum(recv_ref[4 * h + k, 0:PIECE] for k in range(4)) for h in range(2)]
    kept_ref[0] = halves[0]
    kept_ref[1] = halves[1]
    second = sum(recv_ref[k, PIECE : 2 * PIECE] for k in range(N_Y))
    third = mm_exact(second, blocks_ref[2])
    fourth = mm_exact(third, blocks_ref[3])
    for peer in range(N_Z):
        same_pair = (z // 2) == (peer // 2)
        same_octet = (z // 8) == (peer // 8)
        send_ref[peer] = jnp.where(same_pair, second, jnp.where(same_octet, third, fourth))


def far_kernel(z_ref, recv_ref, blocks_ref, kept_ref, send_ref):
    z = z_ref[0]
    zero = jnp.zeros((PIECE, N), F32)
    second, third, fourth = zero, zero, zero
    for peer in range(N_Z):
        same_pair = (z // 2) == (peer // 2)
        same_octet = (z // 8) == (peer // 8)
        value = recv_ref[peer]
        second = second + jnp.where(same_pair, value, zero)
        third = third + jnp.where(same_octet & jnp.logical_not(same_pair), value, zero)
        fourth = fourth + jnp.where(same_octet, zero, value)
    third = third + mm_exact(second, blocks_ref[2])
    fourth = fourth + mm_exact(third, blocks_ref[3])
    fifth = mm_exact(fourth, blocks_ref[4])
    kept_ref[0] = second
    kept_ref[1] = third
    kept_ref[2] = fourth
    for peer in range(N_OUTER):
        send_ref[peer] = fifth


def join_kernel(recv_ref, halves_ref, kept_ref, send_ref):
    fifth = sum(recv_ref[k] for k in range(N_OUTER))
    for y in range(N_Y):
        send_ref[y, 0:PIECE] = halves_ref[y // 4]
        for level in range(3):
            send_ref[y, (level + 1) * PIECE : (level + 2) * PIECE] = kept_ref[level]
        send_ref[y, 4 * PIECE : 5 * PIECE] = fifth


def prepare_kernel(tri_ref, g_ref, blocks_ref, tris_ref, root_ref, link_ref, gain_ref, inverse_ref, base_ref, top_ref):
    leaf = tri_ref[...]
    tris = [leaf] + [tris_ref[level].astype(F32) for level in range(LEVELS)]
    inverses = [tri_inverse(tri) for tri in tris]
    paths = [None] * (LEVELS + 1)
    paths[LEVELS - 1] = blocks_ref[LEVELS - 1].astype(F32)
    for level in reversed(range(LEVELS - 1)):
        paths[level] = mm(blocks_ref[level].astype(F32), paths[level + 1])
    for level in reversed(range(LEVELS)):
        link = mm(tris[level], inverses[level + 1])
        link_ref[level] = link
        if level == LEVELS - 1:
            gain_ref[level] = link - paths[level]
        else:
            gain_ref[level] = mm(link, paths[level + 1]) - paths[level]
    inverse_ref[...] = inverses[0]
    base_ref[...] = mm(g_ref[...], mm(inverses[0], paths[0]), NT)
    top_ref[...] = mm(tris[LEVELS], root_ref[...], NT)


def descend_kernel(recv_ref, sums_ref, q_ref, blocks_ref, link_ref, gain_ref, inverse_ref, base_ref, top_ref, out_ref):
    def gathered(level):
        return jnp.concatenate(
            [recv_ref[y, (level - 1) * PIECE : level * PIECE] for y in range(N_Y)], axis=0
        )

    middle = top_ref[...] - gathered(LEVELS)
    for level in reversed(range(LEVELS)):
        own = gathered(level) if level else sums_ref[...]
        spread = mm(link_ref[level], mirror_lower(middle))
        middle = mm(gain_ref[level], own) + mm_exact(spread, blocks_ref[level], NT)
    inner = mm(q_ref[...], mirror_lower(middle))
    out_ref[...] = base_ref[...] + mm(inner, inverse_ref[...], NT)


def f32(*shape):
    return jax.ShapeDtypeStruct(shape, F32)


SMEM = pl.BlockSpec(memory_space=pltpu.SMEM)
VMEM = pl.BlockSpec(memory_space=pltpu.VMEM)


def on_device(leaf_q, q_cot, leaf_tri, node_blocks, node_tri, root_cot):
    z = lax.axis_index("z").astype(jnp.int32).reshape(1)
    sums, send = pl.pallas_call(
        leaf_kernel, out_shape=(f32(N, N), f32(N_Y, 2 * PIECE, N)), name="leaf"
    )(leaf_q, q_cot, node_blocks)
    recv = lax.all_to_all(send, "y", 0, 0)
    halves, send = pl.pallas_call(
        near_kernel,
        in_specs=[SMEM, VMEM, VMEM],
        out_shape=(f32(2, PIECE, N), f32(N_Z, PIECE, N)),
        name="near",
    )(z, recv, node_blocks)
    recv = lax.all_to_all(send, "z", 0, 0)
    kept, send = pl.pallas_call(
        far_kernel,
        in_specs=[SMEM, VMEM, VMEM],
        out_shape=(f32(3, PIECE, N), f32(N_OUTER, PIECE, N)),
        name="far",
    )(z, recv, node_blocks)
    recv = lax.all_to_all(send, "outer", 0, 0)
    send = pl.pallas_call(join_kernel, out_shape=f32(N_Y, 5 * PIECE, N), name="join")(recv, halves, kept)
    recv = lax.all_to_all(send, "y", 0, 0)
    link, gain, inverse, base, top = pl.pallas_call(
        prepare_kernel,
        out_shape=(f32(LEVELS, N, N), f32(LEVELS, N, N), f32(N, N), f32(ROWS, N), f32(N, N)),
        name="prepare",
    )(leaf_tri, q_cot, node_blocks, node_tri, root_cot)
    return pl.pallas_call(descend_kernel, out_shape=f32(ROWS, N), name="descend")(
        recv, sums, leaf_q, node_blocks, link, gain, inverse, base, top
    )


def solution(mesh):
    split = Mesh(mesh.devices.reshape(N_OUTER, N_Z, N_Y), ("outer", "z", "y"))
    every = ("outer", "z", "y")
    return jax.shard_map(
        on_device,
        mesh=split,
        in_specs=(
            P(every, None),
            P(every, None),
            P(every, None),
            P(None, every, None),
            P(None, every, None),
            P(),
        ),
        out_specs=P(every, None),
        check_vma=False,
    )
```

time: 265 us -> 90.4 us (0.34); the launches traced: 260 us -> 89.8 us
  waiting for transfers between devices: 101 us -> 9.65 us
  matrix products: 72.3 us -> 0 us
  blocking collectives: 0 us -> 43.7 us
  starting transfers between devices: 48.2 us -> 11.1 us
  Pallas kernels: 0 us -> 24 us
  local copies, waits for them, and re-layouts: 23.5 us -> 1.37 us
  between operations: 15.1 us -> 0.02 us
    psum x1 -> x0, waiting for transfers between devices: 89.3 us -> none  [on_device(): top_sum = lax.psum(top_part, 'outer')]
    dot_general x266 -> x0, matrix products: 72.3 us -> none  [the longest x260 69.4 us: matmul(): jnp.dot(left_side, right_side, precision=lax.Precision.HIGHEST, preferred...]
    ppermute x7 -> x0, starting transfers between devices: 48.2 us -> none  [partner(): return lax.ppermute(value, axis, pairs)]
    all_to_all x0 -> x2, blocking collectives: none -> 43.7 us  [the longest x1 30.5 us: on_device(): recv = lax.all_to_all(send, 'z', 0, 0)]
    pallas_call x0 -> x6, Pallas kernels: none -> 24 us  [the longest x1 11.1 us: on_device(): pl.pallas_call(prepare_kernel, out_shape=(f32(LEVELS, N, N), f32(LEVELS,...]
    gather x24 -> x0, local copies, waits for them, and re-layouts: 17.6 us -> none  [small_inverse(): diag_vals = jnp.diagonal(block)]
    ppermute x7 -> x0, waiting for transfers between devices: 11.2 us -> none  [partner(): return lax.ppermute(value, axis, pairs)]
    all_to_all x0 -> x2, starting transfers between devices: none -> 11.1 us  [on_device(): recv = lax.all_to_all(send, 'y', 0, 0)]
  transfers between devices with their start and end apart: 8 -> 2, of which waited for: 7 -> 2; matrix products, arithmetic and copies ran while one was open for 32% -> 0% of each run, Pallas kernels for 0% -> 12%
where the time goes in v1:
time: 90.4 us; the launch traced here: 89.8 us
  blocking collectives  43.7 us (48%)
  Pallas kernels  24 us (27%)
  starting transfers between devices  11.1 us (12%)
  waiting for transfers between devices  9.65 us (11%)
  local copies, waits for them, and re-layouts  1.37 us (2%)
    all_to_all x1, blocking collectives, on_device(): recv = lax.all_to_all(send, 'z', 0, 0)  30.5 us
    all_to_all x1, blocking collectives, on_device(): recv = lax.all_to_all(send, 'outer', 0, 0)  13.2 us
    pallas_call x1, Pallas kernels, on_device(): pl.pallas_call(prepare_kernel, out_shape=(f32(LEVELS, N, N), f32(LEVELS,...  11.1 us
    all_to_all x2, starting transfers between devices, on_device(): recv = lax.all_to_all(send, 'y', 0, 0)  11.1 us
    all_to_all x2, waiting for transfers between devices, on_device(): recv = lax.all_to_all(send, 'y', 0, 0)  9.65 us
    pallas_call x1, Pallas kernels, on_device(): pl.pallas_call(descend_kernel, out_shape=f32(ROWS, N), name='descend')  5.07 us
    pallas_call x1, Pallas kernels, on_device(): pl.pallas_call(leaf_kernel, out_shape=(f32(N, N), f32(N_Y, 2 * PIECE, N))...  2.3 us
    pallas_call x1, Pallas kernels, on_device(): pl.pallas_call(far_kernel, in_specs=[SMEM, VMEM, VMEM], out_shape=(f32(3,...  2.02 us
  transfers between devices with their start and end apart: 2, of which 2 were waited for; matrix products, arithmetic and copies ran while one was open for 0% of the time, Pallas kernels for 12%

profile of v1, /device:TPU:1, one launch (start us, length us, event | category | flops | bytes accessed | tf_op | source)
XLA Modules:
  0.0 89.8 jit_solution(16790972768913380939)
XLA Ops:
  0.0 2.3 %leaf.1 = (f32[128,128]{1,0:T(8,128)}, f32[8,32,128]{2,1,0:T(8,128)}) custom-call(f32[256,128]{1,0:T(8,128)} %q_ref.3, f32[256,128]{1,0:T(8,128)} %g_ref.3, bf16[5,128,128]{2,1,0:T(8,128)(2,1)} %blocks_ref.9), custom_call_target="tpu_custom_call" | custom-call | tf_op jit(solution)/shard_map/leaf/pallas_call | solution.py:210
  2.3 7.6 %all-to-all-start = ((f32[8,32,128]{2,1,0:T(8,128)}), f32[8,32,128]{2,1,0:T(8,128)S(1)}, u32[]{:S(2)}, u32[]{:S(2)}) async-start(f32[8,32,128]{2,1,0:T(8,128)} %get-tuple-element.16), calls=%async_computation | async-start | bytes 262144 | tf_op jit(solution)/shard_map/all_to_all | solution.py:213
  9.9 7.9 %all-to-all-done.recv_ref = f32[8,32,128]{2,1,0:T(8,128)S(1)} async-done(((f32[8,32,128]{2,1,0:T(8,128)}), f32[8,32,128]{2,1,0:T(8,128)S(1)}, u32[]{:S(2)}, u32[]{:S(2)}) %all-to-all-start) | async-done | bytes 131104 | tf_op jit(solution)/shard_map/all_to_all | solution.py:213
  17.9 0.0 copy-start.1
  17.9 0.7 copy-done.1
  18.5 1.9 %near.1 = (f32[2,16,128]{2,1,0:T(8,128)}, f32[16,16,128]{2,1,0:T(8,128)}) custom-call(s32[1]{0:T(128)} %bitcast.z_ref, f32[8,32,128]{2,1,0:T(8,128)} %copy-done.1, bf16[5,128,128]{2,1,0:T(8,128)(2,1)} %blocks_ref.9), custom_call_target="tpu_custom_call" | custom-call | tf_op jit(solution)/shard_map/near/pallas_call | solution.py:214
  20.4 30.5 %all_to_all.20.recv_ref = f32[16,16,128]{2,1,0:T(8,128)} all-to-all(f32[16,16,128]{2,1,0:T(8,128)} %get-tuple-element.17), channel_id=1, replica_groups=mesh['outer'=8,'z'=16,'y'=8] {'z'}, dimensions={0} | all-to-all | bytes 262144 | tf_op jit(solution)/shard_map/all_to_all | solution.py:220
  50.9 2.0 %far.1 = (f32[3,16,128]{2,1,0:T(8,128)}, f32[8,16,128]{2,1,0:T(8,128)}) custom-call(s32[1]{0:T(128)} %bitcast.z_ref, f32[16,16,128]{2,1,0:T(8,128)} %all_to_all.20.recv_ref, bf16[5,128,128]{2,1,0:T(8,128)(2,1)} %blocks_ref.9), custom_call_target="tpu_custom_call" | custom-call | tf_op jit(solution)/shard_map/far/pallas_call | solution.py:221
  53.0 13.2 %all_to_all.21.recv_ref = f32[8,16,128]{2,1,0:T(8,128)} all-to-all(f32[8,16,128]{2,1,0:T(8,128)} %get-tuple-element.18), channel_id=1, replica_groups=mesh['outer'=8,'z'=16,'y'=8] {'outer'}, dimensions={0} | all-to-all | bytes 131072 | tf_op jit(solution)/shard_map/all_to_all | solution.py:227
  66.2 1.6 %join.1 = f32[8,80,128]{2,1,0:T(8,128)} custom-call(f32[8,16,128]{2,1,0:T(8,128)} %all_to_all.21.recv_ref, f32[2,16,128]{2,1,0:T(8,128)} %get-tuple-element.19.halves_ref, f32[3,16,128]{2,1,0:T(8,128)} %get-tuple-element.20.kept_ref), custom_call_target="tpu_custom_call" | custom-call | tf_op jit(solution)/shard_map/join/pallas_call | solution.py:228
  67.7 3.4 %all-to-all-start.3 = ((f32[8,80,128]{2,1,0:T(8,128)}), f32[8,80,128]{2,1,0:T(8,128)S(1)}, u32[]{:S(2)}, u32[]{:S(2)}) async-start(f32[8,80,128]{2,1,0:T(8,128)} %join.1), calls=%async_computation.3 | async-start | bytes 655360 | tf_op jit(solution)/shard_map/all_to_all | solution.py:229
  71.2 11.1 %prepare.1 = (f32[5,128,128]{2,1,0:T(8,128)}, f32[5,128,128]{2,1,0:T(8,128)}, f32[128,128]{1,0:T(8,128)}, f32[256,128]{1,0:T(8,128)}, f32[128,128]{1,0:T(8,128)}) custom-call(f32[128,128]{1,0:T(8,128)} %tri_ref.1, f32[256,128]{1,0:T(8,128)} %g_ref.3, bf16[5,128,128]{2,1,0:T(8,128)(2,1)} %blocks_ref.9, bf16[5,128,128]{2,1,0:T(8,128)(2,1)} %tris_ref.1, ...), custom_call_target="tpu_custom_call" | custom-call | tf_op jit(solution)/shard_map/prepare/pallas_call | solution.py:230
  82.3 1.7 %all-to-all-done.3.recv_ref = f32[8,80,128]{2,1,0:T(8,128)S(1)} async-done(((f32[8,80,128]{2,1,0:T(8,128)}), f32[8,80,128]{2,1,0:T(8,128)S(1)}, u32[]{:S(2)}, u32[]{:S(2)}) %all-to-all-start.3) | async-done | bytes 327712 | tf_op jit(solution)/shard_map/all_to_all | solution.py:229
  84.0 0.0 copy-start
  84.0 0.7 copy-done
  84.8 5.1 %descend.1 = f32[256,128]{1,0:T(8,128)} custom-call(f32[8,80,128]{2,1,0:T(8,128)} %copy-done, f32[128,128]{1,0:T(8,128)} %get-tuple-element.21.sums_ref, f32[256,128]{1,0:T(8,128)} %q_ref.3, bf16[5,128,128]{2,1,0:T(8,128)(2,1)} %blocks_ref.9, f32[5,128,128]{2,1,0:T(8,128)} %get-tuple-element.22.link_ref, f32[5,128,128]{2,1,0:T(8,128)} %get-tuple-element.23.gain_ref, ...), custom_call_target="tpu_custom_call" | custom-call | tf_op jit(solution)/shard_map/descend/pallas_call | solution.py:235
Async XLA Ops:
  2.3 15.6 %all-to-all-start = ((f32[8,32,128]{2,1,0:T(8,128)}), f32[8,32,128]{2,1,0:T(8,128)S(1)}, u32[]{:S(2)}, u32[]{:S(2)}) async-start(f32[8,32,128]{2,1,0:T(8,128)} %get-tuple-element.16), calls=%async_computation | async-start | bytes 262144 | tf_op jit(solution)/shard_map/all_to_all | solution.py:213
  17.9 0.7 copy-start.1
  67.7 16.3 %all-to-all-start.3 = ((f32[8,80,128]{2,1,0:T(8,128)}), f32[8,80,128]{2,1,0:T(8,128)S(1)}, u32[]{:S(2)}, u32[]{:S(2)}) async-start(f32[8,80,128]{2,1,0:T(8,128)} %join.1), calls=%async_computation.3 | async-start | bytes 655360 | tf_op jit(solution)/shard_map/all_to_all | solution.py:229
  84.0 0.7 copy-start

commit v2 on v1

--- a/solution.py
+++ b/solution.py
@@ -103,16 +103,21 @@
     return jnp.concatenate([upper, pair_inverse[64:]], axis=0)
 
 
-def leaf_values(leaf_q, q_cot, block_1, block_2):
-    sums_t = mm(q_cot.T, leaf_q)
-    first_t = mm_exact(sums_t, block_1)
-    second_t = mm_exact(first_t, block_2)
-    return sums_t, first_t, second_t
-
-
-def leaf_kernel(q_ref, g_ref, blocks_ref, sums_ref, send_ref):
-    sums_t, first_t, second_t = leaf_values(q_ref[...], g_ref[...], blocks_ref[0], blocks_ref[1])
+def leaf_kernel(q_hbm, g_hbm, blocks_hbm, sums_ref, send_ref, q_ref, g_ref, blocks_ref, sems):
+    copies = [
+        pltpu.make_async_copy(g_hbm, g_ref, sems.at[0]),
+        pltpu.make_async_copy(q_hbm, q_ref, sems.at[1]),
+        pltpu.make_async_copy(blocks_hbm.at[0:2], blocks_ref, sems.at[2]),
+    ]
+    for copy in copies:
+        copy.start()
+    copies[0].wait()
+    copies[1].wait()
+    sums_t = mm(g_ref[...].T, q_ref[...])
     sums_ref[...] = sums_t
+    copies[2].wait()
+    first_t = mm_exact(sums_t, blocks_ref[0])
+    second_t = mm_exact(first_t, blocks_ref[1])
     for y in range(N_Y):
         send_ref[y, 0:PIECE] = first_t[y * PIECE : (y + 1) * PIECE]
         send_ref[y, PIECE : 2 * PIECE] = second_t[y * PIECE : (y + 1) * PIECE]
@@ -132,7 +137,7 @@
         send_ref[peer] = jnp.where(same_pair, second, jnp.where(same_octet, third, fourth))
 
 
-def far_kernel(z_ref, recv_ref, blocks_ref, kept_ref, send_ref):
+def far_kernel(z_ref, recv_ref, blocks_ref, after_ref, kept_ref, send_ref):
     z = z_ref[0]
     zero = jnp.zeros((PIECE, N), F32)
     second, third, fourth = zero, zero, zero
@@ -153,7 +158,7 @@
         send_ref[peer] = fifth
 
 
-def join_kernel(recv_ref, halves_ref, kept_ref, send_ref):
+def join_kernel(recv_ref, halves_ref, kept_ref, after_ref, send_ref):
     fifth = sum(recv_ref[k] for k in range(N_OUTER))
     for y in range(N_Y):
         send_ref[y, 0:PIECE] = halves_ref[y // 4]
@@ -162,23 +167,26 @@
         send_ref[y, 4 * PIECE : 5 * PIECE] = fifth
 
 
-def prepare_kernel(tri_ref, g_ref, blocks_ref, tris_ref, root_ref, link_ref, gain_ref, inverse_ref, base_ref, top_ref):
-    leaf = tri_ref[...]
-    tris = [leaf] + [tris_ref[level].astype(F32) for level in range(LEVELS)]
-    inverses = [tri_inverse(tri) for tri in tris]
+def inverse_kernel(tri_ref, tris_ref, after_ref, out_ref):
+    tris = [tri_ref[...]] + [tris_ref[level].astype(F32) for level in range(LEVELS)]
+    for level, tri in enumerate(tris):
+        out_ref[level] = tri_inverse(tri)
+
+
+def chain_kernel(tri_ref, g_ref, blocks_ref, tris_ref, root_ref, inverse_ref, after_ref, link_ref, gain_ref, base_ref, top_ref):
+    tris = [tri_ref[...]] + [tris_ref[level].astype(F32) for level in range(LEVELS)]
     paths = [None] * (LEVELS + 1)
     paths[LEVELS - 1] = blocks_ref[LEVELS - 1].astype(F32)
     for level in reversed(range(LEVELS - 1)):
         paths[level] = mm(blocks_ref[level].astype(F32), paths[level + 1])
     for level in reversed(range(LEVELS)):
-        link = mm(tris[level], inverses[level + 1])
+        link = mm(tris[level], inverse_ref[level + 1])
         link_ref[level] = link
         if level == LEVELS - 1:
             gain_ref[level] = link - paths[level]
         else:
             gain_ref[level] = mm(link, paths[level + 1]) - paths[level]
-    inverse_ref[...] = inverses[0]
-    base_ref[...] = mm(g_ref[...], mm(inverses[0], paths[0]), NT)
+    base_ref[...] = mm(g_ref[...], mm(inverse_ref[0], paths[0]), NT)
     top_ref[...] = mm(tris[LEVELS], root_ref[...], NT)
 
 
@@ -194,46 +202,68 @@
         spread = mm(link_ref[level], mirror_lower(middle))
         middle = mm(gain_ref[level], own) + mm_exact(spread, blocks_ref[level], NT)
     inner = mm(q_ref[...], mirror_lower(middle))
-    out_ref[...] = base_ref[...] + mm(inner, inverse_ref[...], NT)
-
-
-def f32(*shape):
-    return jax.ShapeDtypeStruct(shape, F32)
+    out_ref[...] = base_ref[...] + mm(inner, inverse_ref[0], NT)
+
+
+def kept(*shape):
+    return pltpu.VMEM(shape, F32)
+
+
+def near(value):
+    return pltpu.with_memory_space_constraint(value, pltpu.VMEM)
 
 
 SMEM = pl.BlockSpec(memory_space=pltpu.SMEM)
 VMEM = pl.BlockSpec(memory_space=pltpu.VMEM)
+PLAIN = pl.BlockSpec(memory_space=pltpu.HBM)
+
+
+def call(kernel, outs, specs, name, scratch=()):
+    return pl.pallas_call(
+        kernel,
+        in_specs=specs,
+        out_shape=outs,
+        out_specs=jax.tree.map(lambda _: VMEM, outs),
+        scratch_shapes=scratch,
+        name=name,
+        compiler_params=pltpu.CompilerParams(vmem_limit_bytes=16 << 20),
+    )
 
 
 def on_device(leaf_q, q_cot, leaf_tri, node_blocks, node_tri, root_cot):
     z = lax.axis_index("z").astype(jnp.int32).reshape(1)
-    sums, send = pl.pallas_call(
-        leaf_kernel, out_shape=(f32(N, N), f32(N_Y, 2 * PIECE, N)), name="leaf"
+    blocks, tris = near(node_blocks), near(node_tri)
+    tri, cot, root, rows = near(leaf_tri), near(q_cot), near(root_cot), near(leaf_q)
+    scratch = (
+        kept(ROWS, N),
+        kept(ROWS, N),
+        pltpu.VMEM((2, N, N), BF16),
+        pltpu.SemaphoreType.DMA((3,)),
+    )
+    sums, send = call(
+        leaf_kernel, (kept(N, N), kept(N_Y, 2 * PIECE, N)), [PLAIN] * 3, "leaf", scratch
     )(leaf_q, q_cot, node_blocks)
-    recv = lax.all_to_all(send, "y", 0, 0)
-    halves, send = pl.pallas_call(
-        near_kernel,
-        in_specs=[SMEM, VMEM, VMEM],
-        out_shape=(f32(2, PIECE, N), f32(N_Z, PIECE, N)),
-        name="near",
-    )(z, recv, node_blocks)
-    recv = lax.all_to_all(send, "z", 0, 0)
-    kept, send = pl.pallas_call(
-        far_kernel,
-        in_specs=[SMEM, VMEM, VMEM],
-        out_shape=(f32(3, PIECE, N), f32(N_OUTER, PIECE, N)),
-        name="far",
-    )(z, recv, node_blocks)
-    recv = lax.all_to_all(send, "outer", 0, 0)
-    send = pl.pallas_call(join_kernel, out_shape=f32(N_Y, 5 * PIECE, N), name="join")(recv, halves, kept)
-    recv = lax.all_to_all(send, "y", 0, 0)
-    link, gain, inverse, base, top = pl.pallas_call(
-        prepare_kernel,
-        out_shape=(f32(LEVELS, N, N), f32(LEVELS, N, N), f32(N, N), f32(ROWS, N), f32(N, N)),
-        name="prepare",
-    )(leaf_tri, q_cot, node_blocks, node_tri, root_cot)
-    return pl.pallas_call(descend_kernel, out_shape=f32(ROWS, N), name="descend")(
-        recv, sums, leaf_q, node_blocks, link, gain, inverse, base, top
+    recv = near(lax.all_to_all(send, "y", 0, 0))
+    halves, send = call(near_kernel, (kept(2, PIECE, N), kept(N_Z, PIECE, N)), [SMEM, VMEM, VMEM], "near")(
+        z, recv, blocks
+    )
+    halves = near(halves)
+    inverses = call(inverse_kernel, kept(LEVELS + 1, N, N), [VMEM] * 3, "inverse")(tri, tris, halves)
+    inverses = near(inverses)
+    recv = near(lax.all_to_all(send, "z", 0, 0))
+    mine, send = call(
+        far_kernel, (kept(3, PIECE, N), kept(N_OUTER, PIECE, N)), [SMEM] + [VMEM] * 3, "far"
+    )(z, recv, blocks, inverses)
+    mine = near(mine)
+    link, gain, base, top = call(
+        chain_kernel, (kept(LEVELS, N, N), kept(LEVELS, N, N), kept(ROWS, N), kept(N, N)), [VMEM] * 7, "chain"
+    )(tri, cot, blocks, tris, root, inverses, mine)
+    link, gain, base, top = near(link), near(gain), near(base), near(top)
+    recv = near(lax.all_to_all(send, "outer", 0, 0))
+    send = call(join_kernel, kept(N_Y, 5 * PIECE, N), [VMEM] * 4, "join")(recv, halves, mine, top)
+    recv = near(lax.all_to_all(send, "y", 0, 0))
+    return call(descend_kernel, jax.ShapeDtypeStruct((ROWS, N), F32), [VMEM] * 9, "descend")(
+        recv, near(sums), rows, blocks, link, gain, inverses, base, top
     )
 
 

time: 90.4 us -> 85.3 us (0.944)
  blocking collectives: 43.7 us -> 15.2 us
  starting transfers between devices: 11.1 us -> 34.7 us
  Pallas kernels: 24 us -> 16.9 us
  waiting for transfers between devices: 9.65 us -> 15.2 us
  local copies, waits for them, and re-layouts: 1.37 us -> 2.75 us
    all_to_all x2 -> x1, blocking collectives: 43.7 us -> 15.2 us  [on_device(): recv = near(lax.all_to_all(send, 'y', 0, 0))]
    all_to_all x2 -> x3, starting transfers between devices: 11.1 us -> 34.7 us  [the longest x1 18.5 us: on_device(): recv = near(lax.all_to_all(send, 'z', 0, 0))]
    pallas_call x6 -> x7, Pallas kernels: 24 us -> 16.9 us  [the longest x1 7.79 us: on_device(): call(inverse_kernel, kept(LEVELS + 1, N, N), [VMEM] * 3, 'inverse')]
    all_to_all x2 -> x3, waiting for transfers between devices: 9.65 us -> 15.2 us  [the longest x1 7.93 us: on_device(): recv = near(lax.all_to_all(send, 'y', 0, 0))]
    unnamed x4 -> x18, local copies, waits for them, and re-layouts: 1.37 us -> 2.75 us
  transfers between devices with their start and end apart: 2 -> 3, of which waited for: 2 -> 3; matrix products, arithmetic and copies ran while one was open for 0% -> 0% of each run, Pallas kernels for 12% -> 11%
where the time goes in v2:
time: 85.3 us; the launch traced here: 84.8 us
  starting transfers between devices  34.7 us (41%)
  Pallas kernels  16.9 us (20%)
  waiting for transfers between devices  15.2 us (18%)
  blocking collectives  15.2 us (18%)
  local copies, waits for them, and re-layouts  2.75 us (3%)
    all_to_all x1, starting transfers between devices, on_device(): recv = near(lax.all_to_all(send, 'z', 0, 0))  18.5 us
    all_to_all x1, blocking collectives, on_device(): recv = near(lax.all_to_all(send, 'y', 0, 0))  15.2 us
    all_to_all x1, starting transfers between devices, on_device(): recv = near(lax.all_to_all(send, 'outer', 0, 0))  8.39 us
    all_to_all x1, waiting for transfers between devices, on_device(): recv = near(lax.all_to_all(send, 'y', 0, 0))  7.93 us
    pallas_call x1, Pallas kernels, on_device(): call(inverse_kernel, kept(LEVELS + 1, N, N), [VMEM] * 3, 'inverse')  7.79 us
    all_to_all x1, starting transfers between devices, on_device(): recv = near(lax.all_to_all(send, 'y', 0, 0))  7.78 us
    all_to_all x1, waiting for transfers between devices, on_device(): recv = near(lax.all_to_all(send, 'z', 0, 0))  4.16 us
    pallas_call x1, Pallas kernels, on_device(): call(descend_kernel, jax.ShapeDtypeStruct((ROWS, N), F32), [VMEM] * 9, 'd...  3.7 us
  transfers between devices with their start and end apart: 3, of which 3 were waited for; matrix products, arithmetic and copies ran while one was open for 0% of the time, Pallas kernels for 11%

profile of v2, /device:TPU:1, one launch (start us, length us, event | category | flops | bytes accessed | tf_op | source)
XLA Modules:
  0.0 84.8 jit_solution(9356708982179879664)
XLA Ops:
  0.0 0.9 %copy-done = bf16[5,128,128]{2,1,0:T(8,128)(2,1)S(1)} copy-done((bf16[5,128,128]{2,1,0:T(8,128)(2,1)S(1)}, bf16[5,128,128]{2,1,0:T(8,128)(2,1)}, u32[]{:S(2)}) %copy-start) | copy-done | bytes 163864
  0.9 0.9 %copy-done.3 = f32[256,128]{1,0:T(8,128)S(1)} copy-done((f32[256,128]{1,0:T(8,128)S(1)}, f32[256,128]{1,0:T(8,128)}, u32[]{:S(2)}) %copy-start.3) | copy-done | bytes 131096
  1.8 0.9 %copy-done.5 = f32[256,128]{1,0:T(8,128)S(1)} copy-done((f32[256,128]{1,0:T(8,128)S(1)}, f32[256,128]{1,0:T(8,128)}, u32[]{:S(2)}) %copy-start.5) | copy-done | bytes 131096
  2.7 1.7 %leaf.1 = (f32[128,128]{1,0:T(8,128)S(1)}, f32[8,32,128]{2,1,0:T(8,128)}) custom-call(f32[256,128]{1,0:T(8,128)S(1)} %copy-done.5, f32[256,128]{1,0:T(8,128)S(1)} %copy-done.3, bf16[5,128,128]{2,1,0:T(8,128)(2,1)S(1)} %copy-done), custom_call_target="tpu_custom_call" | custom-call | tf_op jit(solution)/shard_map/leaf/pallas_call | solution.py:243
  4.4 0.0 copy-start.1
  4.5 7.8 %all-to-all-start = ((f32[8,32,128]{2,1,0:T(8,128)}), f32[8,32,128]{2,1,0:T(8,128)S(1)}, u32[]{:S(2)}, u32[]{:S(2)}) async-start(f32[8,32,128]{2,1,0:T(8,128)} %get-tuple-element.15), calls=%async_computation | async-start | bytes 262144 | tf_op jit(solution)/shard_map/all_to_all | solution.py:246
  12.2 7.9 %all-to-all-done.recv_ref = f32[8,32,128]{2,1,0:T(8,128)S(1)} async-done(((f32[8,32,128]{2,1,0:T(8,128)}), f32[8,32,128]{2,1,0:T(8,128)S(1)}, u32[]{:S(2)}, u32[]{:S(2)}) %all-to-all-start) | async-done | bytes 131104 | tf_op jit(solution)/shard_map/all_to_all | solution.py:246
  20.2 0.0 copy-done.1
  20.2 0.9 %near.1 = (f32[2,16,128]{2,1,0:T(8,128)S(1)}, f32[16,16,128]{2,1,0:T(8,128)}) custom-call(s32[1]{0:T(128)} %bitcast.z_ref, f32[8,32,128]{2,1,0:T(8,128)S(1)} %all-to-all-done.recv_ref, bf16[5,128,128]{2,1,0:T(8,128)(2,1)S(1)} %copy-done.1), custom_call_target="tpu_custom_call" | custom-call | tf_op jit(solution)/shard_map/near/pallas_call | solution.py:247
  21.1 18.5 %all-to-all-start.1 = ((f32[16,16,128]{2,1,0:T(8,128)}), f32[16,16,128]{2,1,0:T(8,128)S(1)}, u32[]{:S(2)}, u32[]{:S(2)}) async-start(f32[16,16,128]{2,1,0:T(8,128)} %get-tuple-element.16), calls=%async_computation.1 | async-start | bytes 262144 | tf_op jit(solution)/shard_map/all_to_all | solution.py:253
  39.7 0.0 copy-done.2
  39.7 0.0 copy-done.7
  39.7 7.8 %inverse.1.after_ref.inverse_ref = f32[6,128,128]{2,1,0:T(8,128)S(1)} custom-call(f32[128,128]{1,0:T(8,128)S(1)} %copy-done.7, bf16[5,128,128]{2,1,0:T(8,128)(2,1)S(1)} %copy-done.2, f32[2,16,128]{2,1,0:T(8,128)S(1)} %get-tuple-element.17.after_ref.halves_ref), custom_call_target="tpu_custom_call" | custom-call | tf_op jit(solution)/shard_map/inverse/pallas_call | solution.py:251
  47.5 4.2 %all-to-all-done.1.recv_ref = f32[16,16,128]{2,1,0:T(8,128)S(1)} async-done(((f32[16,16,128]{2,1,0:T(8,128)}), f32[16,16,128]{2,1,0:T(8,128)S(1)}, u32[]{:S(2)}, u32[]{:S(2)}) %all-to-all-start.1) | async-done | bytes 131104 | tf_op jit(solution)/shard_map/all_to_all | solution.py:253
  51.6 1.0 %far.1 = (f32[3,16,128]{2,1,0:T(8,128)S(1)}, f32[8,16,128]{2,1,0:T(8,128)}) custom-call(s32[1]{0:T(128)} %bitcast.z_ref, f32[16,16,128]{2,1,0:T(8,128)S(1)} %all-to-all-done.1.recv_ref, bf16[5,128,128]{2,1,0:T(8,128)(2,1)S(1)} %copy-done.1, f32[6,128,128]{2,1,0:T(8,128)S(1)} %inverse.1.after_ref.inverse_ref), custom_call_target="tpu_custom_call" | custom-call | tf_op jit(solution)/shard_map/far/pallas_call | solution.py:254
  52.7 8.4 %all-to-all-start.2 = ((f32[8,16,128]{2,1,0:T(8,128)}), f32[8,16,128]{2,1,0:T(8,128)S(1)}, u32[]{:S(2)}, u32[]{:S(2)}) async-start(f32[8,16,128]{2,1,0:T(8,128)} %get-tuple-element.18), calls=%async_computation.2 | async-start | bytes 131072 | tf_op jit(solution)/shard_map/all_to_all | solution.py:262
  61.1 0.0 copy-done.8
  61.1 0.0 copy-done.4
  61.1 1.7 %chain.1 = (f32[5,128,128]{2,1,0:T(8,128)S(1)}, f32[5,128,128]{2,1,0:T(8,128)S(1)}, f32[256,128]{1,0:T(8,128)S(1)}, f32[128,128]{1,0:T(8,128)S(1)}) custom-call(f32[128,128]{1,0:T(8,128)S(1)} %copy-done.7, f32[256,128]{1,0:T(8,128)S(1)} %copy-done.4, bf16[5,128,128]{2,1,0:T(8,128)(2,1)S(1)} %copy-done.1, bf16[5,128,128]{2,1,0:T(8,128)(2,1)S(1)} %copy-done.2, ...), custom_call_target="tpu_custom_call" | custom-call | tf_op jit(solution)/shard_map/chain/pallas_call | solution.py:258
  62.8 3.1 %all-to-all-done.2.recv_ref = f32[8,16,128]{2,1,0:T(8,128)S(1)} async-done(((f32[8,16,128]{2,1,0:T(8,128)}), f32[8,16,128]{2,1,0:T(8,128)S(1)}, u32[]{:S(2)}, u32[]{:S(2)}) %all-to-all-start.2) | async-done | bytes 65568 | tf_op jit(solution)/shard_map/all_to_all | solution.py:262
  65.9 0.0 copy-start.6
  66.0 15.2 %all_to_all.20.recv_ref = f32[8,80,128]{2,1,0:T(8,128)S(1)} all-to-all(f32[8,80,128]{2,1,0:T(8,128)S(1)} %join.1), channel_id=1, replica_groups=mesh['outer'=8,'z'=16,'y'=8] {'y'}, dimensions={0} | all-to-all | bytes 655360 | tf_op jit(solution)/shard_map/all_to_all | solution.py:264
  81.1 0.0 copy-done.6
  81.1 3.7 %descend.1 = f32[256,128]{1,0:T(8,128)} custom-call(f32[8,80,128]{2,1,0:T(8,128)S(1)} %all_to_all.20.recv_ref, f32[128,128]{1,0:T(8,128)S(1)} %get-tuple-element.21.sums_ref, f32[256,128]{1,0:T(8,128)S(1)} %copy-done.6, bf16[5,128,128]{2,1,0:T(8,128)(2,1)S(1)} %copy-done.1, f32[5,128,128]{2,1,0:T(8,128)S(1)} %get-tuple-element.22.link_ref, ...), custom_call_target="tpu_custom_call" | custom-call | tf_op jit(solution)/shard_map/descend/pallas_call | solution.py:265
  (8 shorter events, 0.0 us)
Async XLA Ops:
  0.0 0.9 %copy-start = (bf16[5,128,128]{2,1,0:T(8,128)(2,1)S(1)}, bf16[5,128,128]{2,1,0:T(8,128)(2,1)}, u32[]{:S(2)}) copy-start(bf16[5,128,128]{2,1,0:T(8,128)(2,1)} %blocks_ref.7) | copy-start | bytes 491524
  0.9 0.9 %copy-start.3 = (f32[256,128]{1,0:T(8,128)S(1)}, f32[256,128]{1,0:T(8,128)}, u32[]{:S(2)}) copy-start(f32[256,128]{1,0:T(8,128)} %g_ref.1) | copy-start | bytes 393220
  1.8 0.9 %copy-start.5 = (f32[256,128]{1,0:T(8,128)S(1)}, f32[256,128]{1,0:T(8,128)}, u32[]{:S(2)}) copy-start(f32[256,128]{1,0:T(8,128)} %q_ref.1) | copy-start | bytes 393220
  4.4 15.7 %copy-start.1 = (bf16[5,128,128]{2,1,0:T(8,128)(2,1)S(1)}, bf16[5,128,128]{2,1,0:T(8,128)(2,1)}, u32[]{:S(2)}) copy-start(bf16[5,128,128]{2,1,0:T(8,128)(2,1)} %blocks_ref.7) | copy-start | bytes 491524
  4.5 15.7 %all-to-all-start = ((f32[8,32,128]{2,1,0:T(8,128)}), f32[8,32,128]{2,1,0:T(8,128)S(1)}, u32[]{:S(2)}, u32[]{:S(2)}) async-start(f32[8,32,128]{2,1,0:T(8,128)} %get-tuple-element.15), calls=%async_computation | async-start | bytes 262144 | tf_op jit(solution)/shard_map/all_to_all | solution.py:246
  21.1 18.6 %copy-start.2 = (bf16[5,128,128]{2,1,0:T(8,128)(2,1)S(1)}, bf16[5,128,128]{2,1,0:T(8,128)(2,1)}, u32[]{:S(2)}) copy-start(bf16[5,128,128]{2,1,0:T(8,128)(2,1)} %tris_ref.3) | copy-start | bytes 491524
  21.1 18.6 %copy-start.7 = (f32[128,128]{1,0:T(8,128)S(1)}, f32[128,128]{1,0:T(8,128)}, u32[]{:S(2)}) copy-start(f32[128,128]{1,0:T(8,128)} %tri_ref.3) | copy-start | bytes 196612
  21.1 30.5 %all-to-all-start.1 = ((f32[16,16,128]{2,1,0:T(8,128)}), f32[16,16,128]{2,1,0:T(8,128)S(1)}, u32[]{:S(2)}, u32[]{:S(2)}) async-start(f32[16,16,128]{2,1,0:T(8,128)} %get-tuple-element.16), calls=%async_computation.1 | async-start | bytes 262144 | tf_op jit(solution)/shard_map/all_to_all | solution.py:253
  51.6 9.4 %copy-start.8 = (f32[128,128]{1,0:T(8,128)S(1)}, f32[128,128]{1,0:T(8,128)}, u32[]{:S(2)}) copy-start(f32[128,128]{1,0:T(8,128)} %root_ref.1) | copy-start | bytes 196612
  52.7 8.4 %copy-start.4 = (f32[256,128]{1,0:T(8,128)S(1)}, f32[256,128]{1,0:T(8,128)}, u32[]{:S(2)}) copy-start(f32[256,128]{1,0:T(8,128)} %g_ref.1) | copy-start | bytes 393220
  52.7 13.2 %all-to-all-start.2 = ((f32[8,16,128]{2,1,0:T(8,128)}), f32[8,16,128]{2,1,0:T(8,128)S(1)}, u32[]{:S(2)}, u32[]{:S(2)}) async-start(f32[8,16,128]{2,1,0:T(8,128)} %get-tuple-element.18), calls=%async_computation.2 | async-start | bytes 131072 | tf_op jit(solution)/shard_map/all_to_all | solution.py:262
  65.9 15.2 %copy-start.6 = (f32[256,128]{1,0:T(8,128)S(1)}, f32[256,128]{1,0:T(8,128)}, u32[]{:S(2)}) copy-start(f32[256,128]{1,0:T(8,128)} %q_ref.1) | copy-start | bytes 393220

commit v3 on v2

--- a/solution.py
+++ b/solution.py
@@ -34,15 +34,19 @@
 NT = ((1,), (1,))
 
 
-def mm(left, right, dims=NN):
-    rows = left.shape[0]
-    lh, lm, ll = split3(left)
-    rh, rm, rl = split3(right)
+def mm_parts(left, right, dims=NN):
+    lh, lm, ll = left
+    rh, rm, rl = right
+    rows = lh.shape[0]
     first = dot(jnp.concatenate([lh, lm, ll], axis=0), rh, dims)
     second = dot(jnp.concatenate([lh, lm], axis=0), rm, dims)
     third = dot(lh, rl, dims)
     small = first[2 * rows :] + second[rows:] + third
     return first[:rows] + (first[rows : 2 * rows] + second[:rows] + small)
+
+
+def mm(left, right, dims=NN):
+    return mm_parts(split3(left), split3(right), dims)
 
 
 def mm_exact(left, right, dims=NN):
@@ -72,33 +76,44 @@
     same = (row // BLOCK) == (col // BLOCK)
     strict = jnp.where(same & (row < col), -triangle, 0.0) / diag_col
 
+    same_half = jnp.where(same, 1.0, 0.0).astype(BF16) > 0
+    pair_half = jnp.where(row // 64 == col // 64, 1.0, 0.0).astype(BF16) > 0
+    zero = jnp.zeros((N, N), BF16)
+
     def packed(matrix):
         return (matrix[0:32] + matrix[32:64]) + (matrix[64:96] + matrix[96:128])
 
-    def spread(rows):
-        return jnp.where(same, jnp.concatenate([rows] * 4, axis=0), 0.0)
+    def spread(parts, mask, copies):
+        return [jnp.where(mask, jnp.concatenate([part] * copies, axis=0), zero) for part in parts]
+
+    def stacked(parts, others):
+        return [jnp.concatenate([part, other], axis=0) for part, other in zip(parts, others)]
 
     small_row, small_col = iotas(BLOCK)
     eye = jnp.where(small_row == small_col % BLOCK, 1.0, 0.0).astype(F32)
     power = packed(strict)
     product = eye + power
-    power = mm(power, strict)
+    parts = split3(power)
+    power = mm_parts(parts, spread(parts, same_half, 4))
     for _ in range(3):
-        both = mm(jnp.concatenate([power, product], axis=0), spread(power))
+        parts = split3(power)
+        both = mm_parts(stacked(parts, split3(product)), spread(parts, same_half, 4))
         product = product + both[BLOCK:]
         power = both[:BLOCK]
-    product = product + mm(product, spread(power))
+    parts = split3(power)
+    product = product + mm_parts(split3(product), spread(parts, same_half, 4))
     inverse = product / diag_row
-    block_inverse = spread(inverse)
+    parts = split3(inverse)
     corner = jnp.where((row // 64 == col // 64) & (row // 32 < col // 32), triangle, 0.0)
-    linked = mm(mm(inverse, corner), block_inverse)
+    linked = mm_parts(split3(mm_parts(parts, split3(corner))), spread(parts, same_half, 4))
     odd = (small_col // BLOCK) % 2 == 1
     top = jnp.where(odd, -linked, inverse)
     bottom = jnp.where(odd, inverse, 0.0)
     pair = jnp.concatenate([top, bottom], axis=0)
     pair_inverse = jnp.where(row // 64 == col // 64, jnp.concatenate([pair, pair], axis=0), 0.0)
+    parts = split3(pair)
     corner = jnp.where(row // 64 < col // 64, triangle, 0.0)
-    linked = mm(mm(pair, corner), pair_inverse)
+    linked = mm_parts(split3(mm_parts(parts, split3(corner))), spread(parts, pair_half, 2))
     upper = pair_inverse[:64] - linked
     return jnp.concatenate([upper, pair_inverse[64:]], axis=0)
 
@@ -123,7 +138,7 @@
         send_ref[y, PIECE : 2 * PIECE] = second_t[y * PIECE : (y + 1) * PIECE]
 
 
-def near_kernel(z_ref, recv_ref, blocks_ref, kept_ref, send_ref):
+def near_kernel(z_ref, recv_ref, blocks_ref, after_ref, kept_ref, send_ref):
     z = z_ref[0]
     halves = [sum(recv_ref[4 * h + k, 0:PIECE] for k in range(4)) for h in range(2)]
     kept_ref[0] = halves[0]
@@ -158,7 +173,7 @@
         send_ref[peer] = fifth
 
 
-def join_kernel(recv_ref, halves_ref, kept_ref, after_ref, send_ref):
+def join_kernel(recv_ref, halves_ref, kept_ref, send_ref):
     fifth = sum(recv_ref[k] for k in range(N_OUTER))
     for y in range(N_Y):
         send_ref[y, 0:PIECE] = halves_ref[y // 4]
@@ -167,42 +182,47 @@
         send_ref[y, 4 * PIECE : 5 * PIECE] = fifth
 
 
-def inverse_kernel(tri_ref, tris_ref, after_ref, out_ref):
-    tris = [tri_ref[...]] + [tris_ref[level].astype(F32) for level in range(LEVELS)]
-    for level, tri in enumerate(tris):
-        out_ref[level] = tri_inverse(tri)
-
-
-def chain_kernel(tri_ref, g_ref, blocks_ref, tris_ref, root_ref, inverse_ref, after_ref, link_ref, gain_ref, base_ref, top_ref):
+def low_inverse_kernel(tri_ref, tris_ref, after_ref, out_ref):
+    out_ref[0] = tri_inverse(tri_ref[...])
+    for level in range(2):
+        out_ref[level + 1] = tri_inverse(tris_ref[level].astype(F32))
+
+
+def high_inverse_kernel(tris_ref, after_ref, out_ref):
+    for level in range(3):
+        out_ref[level] = tri_inverse(tris_ref[level + 2].astype(F32))
+
+
+def chain_kernel(tri_ref, g_ref, blocks_ref, tris_ref, root_ref, low_ref, high_ref, link_ref, gain_ref, base_ref, top_ref):
     tris = [tri_ref[...]] + [tris_ref[level].astype(F32) for level in range(LEVELS)]
     paths = [None] * (LEVELS + 1)
     paths[LEVELS - 1] = blocks_ref[LEVELS - 1].astype(F32)
     for level in reversed(range(LEVELS - 1)):
         paths[level] = mm(blocks_ref[level].astype(F32), paths[level + 1])
     for level in reversed(range(LEVELS)):
-        link = mm(tris[level], inverse_ref[level + 1])
+        link = mm(tris[level], low_ref[level + 1] if level < 2 else high_ref[level - 2])
         link_ref[level] = link
         if level == LEVELS - 1:
             gain_ref[level] = link - paths[level]
         else:
             gain_ref[level] = mm(link, paths[level + 1]) - paths[level]
-    base_ref[...] = mm(g_ref[...], mm(inverse_ref[0], paths[0]), NT)
+    base_ref[...] = mm(g_ref[...], mm(low_ref[0], paths[0]), NT)
     top_ref[...] = mm(tris[LEVELS], root_ref[...], NT)
 
 
-def descend_kernel(recv_ref, sums_ref, q_ref, blocks_ref, link_ref, gain_ref, inverse_ref, base_ref, top_ref, out_ref):
-    def gathered(level):
-        return jnp.concatenate(
-            [recv_ref[y, (level - 1) * PIECE : level * PIECE] for y in range(N_Y)], axis=0
-        )
-
-    middle = top_ref[...] - gathered(LEVELS)
+def gathered(recv_ref, slot):
+    pieces = [recv_ref[y, slot * PIECE : (slot + 1) * PIECE] for y in range(N_Y)]
+    return jnp.concatenate(pieces, axis=0)
+
+
+def descend_kernel(recv_ref, sums_ref, q_ref, blocks_ref, link_ref, gain_ref, low_ref, base_ref, top_ref, out_ref):
+    middle = top_ref[...] - gathered(recv_ref, LEVELS - 1)
     for level in reversed(range(LEVELS)):
-        own = gathered(level) if level else sums_ref[...]
+        own = gathered(recv_ref, level - 1) if level else sums_ref[...]
         spread = mm(link_ref[level], mirror_lower(middle))
         middle = mm(gain_ref[level], own) + mm_exact(spread, blocks_ref[level], NT)
     inner = mm(q_ref[...], mirror_lower(middle))
-    out_ref[...] = base_ref[...] + mm(inner, inverse_ref[0], NT)
+    out_ref[...] = base_ref[...] + mm(inner, low_ref[0], NT)
 
 
 def kept(*shape):
@@ -211,6 +231,10 @@
 
 def near(value):
     return pltpu.with_memory_space_constraint(value, pltpu.VMEM)
+
+
+def far_away(value):
+    return pltpu.with_memory_space_constraint(value, pltpu.HBM)
 
 
 SMEM = pl.BlockSpec(memory_space=pltpu.SMEM)
@@ -232,8 +256,6 @@
 
 def on_device(leaf_q, q_cot, leaf_tri, node_blocks, node_tri, root_cot):
     z = lax.axis_index("z").astype(jnp.int32).reshape(1)
-    blocks, tris = near(node_blocks), near(node_tri)
-    tri, cot, root, rows = near(leaf_tri), near(q_cot), near(root_cot), near(leaf_q)
     scratch = (
         kept(ROWS, N),
         kept(ROWS, N),
@@ -242,28 +264,35 @@
     )
     sums, send = call(
         leaf_kernel, (kept(N, N), kept(N_Y, 2 * PIECE, N)), [PLAIN] * 3, "leaf", scratch
-    )(leaf_q, q_cot, node_blocks)
+    )(far_away(leaf_q), far_away(q_cot), far_away(node_blocks))
+    sums = near(sums)
+    blocks, tris = near(node_blocks), near(node_tri)
+    tri, cot, root, rows = near(leaf_tri), near(q_cot), near(root_cot), near(leaf_q)
+
     recv = near(lax.all_to_all(send, "y", 0, 0))
-    halves, send = call(near_kernel, (kept(2, PIECE, N), kept(N_Z, PIECE, N)), [SMEM, VMEM, VMEM], "near")(
-        z, recv, blocks
-    )
+    low = near(call(low_inverse_kernel, kept(3, N, N), [VMEM] * 3, "low")(tri, tris, sums))
+    halves, send = call(
+        near_kernel, (kept(2, PIECE, N), kept(N_Z, PIECE, N)), [SMEM] + [VMEM] * 3, "near"
+    )(z, recv, blocks, low)
     halves = near(halves)
-    inverses = call(inverse_kernel, kept(LEVELS + 1, N, N), [VMEM] * 3, "inverse")(tri, tris, halves)
-    inverses = near(inverses)
+
     recv = near(lax.all_to_all(send, "z", 0, 0))
+    high = near(call(high_inverse_kernel, kept(3, N, N), [VMEM] * 2, "high")(tris, halves))
+    link, gain, base, top = call(
+        chain_kernel, (kept(LEVELS, N, N), kept(LEVELS, N, N), kept(ROWS, N), kept(N, N)), [VMEM] * 7, "chain"
+    )(tri, cot, blocks, tris, root, low, high)
+    link, gain, base, top = near(link), near(gain), near(base), near(top)
     mine, send = call(
         far_kernel, (kept(3, PIECE, N), kept(N_OUTER, PIECE, N)), [SMEM] + [VMEM] * 3, "far"
-    )(z, recv, blocks, inverses)
+    )(z, recv, blocks, top)
     mine = near(mine)
-    link, gain, base, top = call(
-        chain_kernel, (kept(LEVELS, N, N), kept(LEVELS, N, N), kept(ROWS, N), kept(N, N)), [VMEM] * 7, "chain"
-    )(tri, cot, blocks, tris, root, inverses, mine)
-    link, gain, base, top = near(link), near(gain), near(base), near(top)
+
     recv = near(lax.all_to_all(send, "outer", 0, 0))
-    send = call(join_kernel, kept(N_Y, 5 * PIECE, N), [VMEM] * 4, "join")(recv, halves, mine, top)
+    send = call(join_kernel, kept(N_Y, 5 * PIECE, N), [VMEM] * 3, "join")(recv, halves, mine)
+
     recv = near(lax.all_to_all(send, "y", 0, 0))
     return call(descend_kernel, jax.ShapeDtypeStruct((ROWS, N), F32), [VMEM] * 9, "descend")(
-        recv, near(sums), rows, blocks, link, gain, inverses, base, top
+        recv, sums, rows, blocks, link, gain, low, base, top
     )
 
 

time: 85.3 us -> 81.4 us (0.954)
  blocking collectives: 15.2 us -> 27.4 us
  starting transfers between devices: 34.7 us -> 26.2 us
  waiting for transfers between devices: 15.2 us -> 9.93 us
  local copies, waits for them, and re-layouts: 2.75 us -> 0.04 us
    all_to_all x0 -> x1, blocking collectives: none -> 12.9 us  [on_device(): recv = near(lax.all_to_all(send, 'outer', 0, 0))]
    all_to_all x1 -> x0, starting transfers between devices: 8.39 us -> none  [on_device(): recv = near(lax.all_to_all(send, 'outer', 0, 0))]
    all_to_all x1, waiting for transfers between devices: 7.93 us -> 3.82 us  [on_device(): recv = near(lax.all_to_all(send, 'y', 0, 0))]
    all_to_all x1 -> x0, waiting for transfers between devices: 3.12 us -> none  [on_device(): recv = near(lax.all_to_all(send, 'outer', 0, 0))]
    unnamed x18 -> x12, local copies, waits for them, and re-layouts: 2.75 us -> 0.04 us
    all_to_all x1, waiting for transfers between devices: 4.16 us -> 6.11 us  [on_device(): recv = near(lax.all_to_all(send, 'z', 0, 0))]
    pallas_call x3 -> x4, Pallas kernels: 8.75 us -> 9.13 us  [the longest x1 4.09 us: on_device(): call(low_inverse_kernel, kept(3, N, N), [VMEM] * 3, 'low')(tri, tris, sums)]
  transfers between devices with their start and end apart: 3 -> 2, of which waited for: 3 -> 2; matrix products, arithmetic and copies ran while one was open for 0% -> 0% of each run, Pallas kernels for 11% -> 12%
where the time goes in v3:
time: 81.4 us; the launch traced here: 80.8 us
  blocking collectives  27.4 us (34%)
  starting transfers between devices  26.2 us (32%)
  Pallas kernels  17.2 us (21%)
  waiting for transfers between devices  9.93 us (12%)
    all_to_all x1, starting transfers between devices, on_device(): recv = near(lax.all_to_all(send, 'z', 0, 0))  18.4 us
    all_to_all x1, blocking collectives, on_device(): recv = near(lax.all_to_all(send, 'y', 0, 0))  14.4 us
    all_to_all x1, blocking collectives, on_device(): recv = near(lax.all_to_all(send, 'outer', 0, 0))  12.9 us
    all_to_all x1, starting transfers between devices, on_device(): recv = near(lax.all_to_all(send, 'y', 0, 0))  7.79 us
    all_to_all x1, waiting for transfers between devices, on_device(): recv = near(lax.all_to_all(send, 'z', 0, 0))  6.11 us
    pallas_call x1, Pallas kernels, on_device(): call(low_inverse_kernel, kept(3, N, N), [VMEM] * 3, 'low')(tri, tris, sums)  4.09 us
    pallas_call x1, Pallas kernels, on_device(): call(high_inverse_kernel, kept(3, N, N), [VMEM] * 2, 'high')(tris, halves)  4.08 us
    all_to_all x1, waiting for transfers between devices, on_device(): recv = near(lax.all_to_all(send, 'y', 0, 0))  3.82 us
  transfers between devices with their start and end apart: 2, of which 2 were waited for; matrix products, arithmetic and copies ran while one was open for 0% of the time, Pallas kernels for 12%

profile of v3, /device:TPU:1, one launch (start us, length us, event | category | flops | bytes accessed | tf_op | source)
XLA Modules:
  0.0 80.8 jit_solution(2637955083519898139)
XLA Ops:
  0.0 2.3 %leaf.1 = (f32[128,128]{1,0:T(8,128)S(1)}, f32[8,32,128]{2,1,0:T(8,128)}) custom-call(f32[256,128]{1,0:T(8,128)} %q_ref.1, f32[256,128]{1,0:T(8,128)} %g_ref.1, bf16[5,128,128]{2,1,0:T(8,128)(2,1)} %blocks_ref.7), custom_call_target="tpu_custom_call" | custom-call | tf_op jit(solution)/shard_map/leaf/pallas_call | solution.py:265
  2.3 0.0 copy-start.1
  2.3 0.0 copy-start.4
  2.3 7.8 %all-to-all-start = ((f32[8,32,128]{2,1,0:T(8,128)}), f32[8,32,128]{2,1,0:T(8,128)S(1)}, u32[]{:S(2)}, u32[]{:S(2)}) async-start(f32[8,32,128]{2,1,0:T(8,128)} %get-tuple-element.15), calls=%async_computation | async-start | bytes 262144 | tf_op jit(solution)/shard_map/all_to_all | solution.py:272
  10.1 0.0 copy-done.1
  10.1 0.0 copy-done.4
  10.1 0.0 copy-start
  10.1 4.1 %low.1.after_ref.low_ref = f32[3,128,128]{2,1,0:T(8,128)S(1)} custom-call(f32[128,128]{1,0:T(8,128)S(1)} %copy-done.4, bf16[5,128,128]{2,1,0:T(8,128)(2,1)S(1)} %copy-done.1, f32[128,128]{1,0:T(8,128)S(1)} %get-tuple-element.16.after_ref.sums_ref), custom_call_target="tpu_custom_call" | custom-call | tf_op jit(solution)/shard_map/low/pallas_call | solution.py:273
  14.2 3.8 %all-to-all-done.recv_ref = f32[8,32,128]{2,1,0:T(8,128)S(1)} async-done(((f32[8,32,128]{2,1,0:T(8,128)}), f32[8,32,128]{2,1,0:T(8,128)S(1)}, u32[]{:S(2)}, u32[]{:S(2)}) %all-to-all-start) | async-done | bytes 131104 | tf_op jit(solution)/shard_map/all_to_all | solution.py:272
  18.0 0.0 copy-done
  18.0 0.9 %near.1 = (f32[2,16,128]{2,1,0:T(8,128)S(1)}, f32[16,16,128]{2,1,0:T(8,128)}) custom-call(s32[1]{0:T(128)} %bitcast.z_ref, f32[8,32,128]{2,1,0:T(8,128)S(1)} %all-to-all-done.recv_ref, bf16[5,128,128]{2,1,0:T(8,128)(2,1)S(1)} %copy-done, f32[3,128,128]{2,1,0:T(8,128)S(1)} %low.1.after_ref.low_ref), custom_call_target="tpu_custom_call" | custom-call | tf_op jit(solution)/shard_map/near/pallas_call | solution.py:274
  19.0 18.4 %all-to-all-start.1 = ((f32[16,16,128]{2,1,0:T(8,128)}), f32[16,16,128]{2,1,0:T(8,128)S(1)}, u32[]{:S(2)}, u32[]{:S(2)}) async-start(f32[16,16,128]{2,1,0:T(8,128)} %get-tuple-element.17), calls=%async_computation.1 | async-start | bytes 262144 | tf_op jit(solution)/shard_map/all_to_all | solution.py:279
  37.4 0.0 copy-start.3
  37.4 0.0 copy-start.5
  37.4 4.1 %high.1.high_ref = f32[3,128,128]{2,1,0:T(8,128)S(1)} custom-call(bf16[5,128,128]{2,1,0:T(8,128)(2,1)S(1)} %copy-done.1, f32[2,16,128]{2,1,0:T(8,128)S(1)} %get-tuple-element.18.after_ref.halves_ref), custom_call_target="tpu_custom_call" | custom-call | tf_op jit(solution)/shard_map/high/pallas_call | solution.py:280
  41.5 0.0 copy-done.3
  41.5 0.0 copy-done.5
  41.5 1.7 %chain.1 = (f32[5,128,128]{2,1,0:T(8,128)S(1)}, f32[5,128,128]{2,1,0:T(8,128)S(1)}, f32[256,128]{1,0:T(8,128)S(1)}, f32[128,128]{1,0:T(8,128)S(1)}) custom-call(f32[128,128]{1,0:T(8,128)S(1)} %copy-done.4, f32[256,128]{1,0:T(8,128)S(1)} %copy-done.3, bf16[5,128,128]{2,1,0:T(8,128)(2,1)S(1)} %copy-done, bf16[5,128,128]{2,1,0:T(8,128)(2,1)S(1)} %copy-done.1, ...), custom_call_target="tpu_custom_call" | custom-call | tf_op jit(solution)/shard_map/chain/pallas_call | solution.py:281
  43.2 6.1 %all-to-all-done.1.recv_ref = f32[16,16,128]{2,1,0:T(8,128)S(1)} async-done(((f32[16,16,128]{2,1,0:T(8,128)}), f32[16,16,128]{2,1,0:T(8,128)S(1)}, u32[]{:S(2)}, u32[]{:S(2)}) %all-to-all-start.1) | async-done | bytes 131104 | tf_op jit(solution)/shard_map/all_to_all | solution.py:279
  49.4 0.4 far.1
  49.7 12.9 %all_to_all.20.recv_ref = f32[8,16,128]{2,1,0:T(8,128)S(1)} all-to-all(f32[8,16,128]{2,1,0:T(8,128)S(1)} %get-tuple-element.20), channel_id=1, replica_groups=mesh['outer'=8,'z'=16,'y'=8] {'outer'}, dimensions={0} | all-to-all | bytes 131072 | tf_op jit(solution)/shard_map/all_to_all | solution.py:290
  62.7 0.0 copy-start.2
  62.7 14.4 %all_to_all.21.recv_ref = f32[8,80,128]{2,1,0:T(8,128)S(1)} all-to-all(f32[8,80,128]{2,1,0:T(8,128)S(1)} %join.1), channel_id=1, replica_groups=mesh['outer'=8,'z'=16,'y'=8] {'y'}, dimensions={0} | all-to-all | bytes 655360 | tf_op jit(solution)/shard_map/all_to_all | solution.py:293
  77.1 3.7 %descend.1 = f32[256,128]{1,0:T(8,128)} custom-call(f32[8,80,128]{2,1,0:T(8,128)S(1)} %all_to_all.21.recv_ref, f32[128,128]{1,0:T(8,128)S(1)} %get-tuple-element.16.after_ref.sums_ref, f32[256,128]{1,0:T(8,128)S(1)} %copy-done.2, bf16[5,128,128]{2,1,0:T(8,128)(2,1)S(1)} %copy-done, f32[5,128,128]{2,1,0:T(8,128)S(1)} %get-tuple-element.22.link_ref, ...), custom_call_target="tpu_custom_call" | custom-call | tf_op jit(solution)/shard_map/descend/pallas_call | solution.py:294
  (2 shorter events, 0.0 us)
Async XLA Ops:
  2.3 7.8 %copy-start.1 = (bf16[5,128,128]{2,1,0:T(8,128)(2,1)S(1)}, bf16[5,128,128]{2,1,0:T(8,128)(2,1)}, u32[]{:S(2)}) copy-start(bf16[5,128,128]{2,1,0:T(8,128)(2,1)} %tris_ref.5) | copy-start | bytes 491524
  2.3 7.8 %copy-start.4 = (f32[128,128]{1,0:T(8,128)S(1)}, f32[128,128]{1,0:T(8,128)}, u32[]{:S(2)}) copy-start(f32[128,128]{1,0:T(8,128)} %tri_ref.3) | copy-start | bytes 196612
  2.3 15.7 %all-to-all-start = ((f32[8,32,128]{2,1,0:T(8,128)}), f32[8,32,128]{2,1,0:T(8,128)S(1)}, u32[]{:S(2)}, u32[]{:S(2)}) async-start(f32[8,32,128]{2,1,0:T(8,128)} %get-tuple-element.15), calls=%async_computation | async-start | bytes 262144 | tf_op jit(solution)/shard_map/all_to_all | solution.py:272
  10.1 7.9 %copy-start = (bf16[5,128,128]{2,1,0:T(8,128)(2,1)S(1)}, bf16[5,128,128]{2,1,0:T(8,128)(2,1)}, u32[]{:S(2)}) copy-start(bf16[5,128,128]{2,1,0:T(8,128)(2,1)} %blocks_ref.7) | copy-start | bytes 491524
  19.0 30.4 %all-to-all-start.1 = ((f32[16,16,128]{2,1,0:T(8,128)}), f32[16,16,128]{2,1,0:T(8,128)S(1)}, u32[]{:S(2)}, u32[]{:S(2)}) async-start(f32[16,16,128]{2,1,0:T(8,128)} %get-tuple-element.17), calls=%async_computation.1 | async-start | bytes 262144 | tf_op jit(solution)/shard_map/all_to_all | solution.py:279
  37.4 4.1 %copy-start.3 = (f32[256,128]{1,0:T(8,128)S(1)}, f32[256,128]{1,0:T(8,128)}, u32[]{:S(2)}) copy-start(f32[256,128]{1,0:T(8,128)} %g_ref.1) | copy-start | bytes 393220
  37.4 4.1 %copy-start.5 = (f32[128,128]{1,0:T(8,128)S(1)}, f32[128,128]{1,0:T(8,128)}, u32[]{:S(2)}) copy-start(f32[128,128]{1,0:T(8,128)} %root_ref.1) | copy-start | bytes 196612
  62.7 14.5 %copy-start.2 = (f32[256,128]{1,0:T(8,128)S(1)}, f32[256,128]{1,0:T(8,128)}, u32[]{:S(2)}) copy-start(f32[256,128]{1,0:T(8,128)} %q_ref.1) | copy-start | bytes 393220

commit v4 on v3

--- a/solution.py
+++ b/solution.py
@@ -56,6 +56,24 @@
     return full[:rows] + (full[rows : 2 * rows] + full[2 * rows :])
 
 
+def split2(value):
+    high = value.astype(BF16)
+    return high, (value - high.astype(F32)).astype(BF16)
+
+
+def mm_short(left, right, dims=NN):
+    lh, ll = split2(left)
+    rh, rl = split2(right)
+    wide = jnp.concatenate([lh, ll, lh], axis=1)
+    return dot(wide, jnp.concatenate([rh, rh, rl], axis=dims[1][0]), dims)
+
+
+def mm_exact_short(left, right, dims=NN):
+    lh, ll = split2(left)
+    wide = jnp.concatenate([ll, lh], axis=1)
+    return dot(wide, jnp.concatenate([right, right], axis=dims[1][0]), dims)
+
+
 def iotas(rows=N):
     return (
         lax.broadcasted_iota(jnp.int32, (rows, N), 0),
@@ -68,17 +86,17 @@
     return jnp.where(row >= col, matrix, matrix.T)
 
 
-def tri_inverse(triangle):
+def tri_inverses(triangles):
     row, col = iotas()
     on_diag = row == col
-    diag_col = jnp.sum(jnp.where(on_diag, triangle, 0.0), axis=1, keepdims=True)
-    diag_row = jnp.sum(jnp.where(on_diag, triangle, 0.0), axis=0, keepdims=True)
-    same = (row // BLOCK) == (col // BLOCK)
-    strict = jnp.where(same & (row < col), -triangle, 0.0) / diag_col
-
-    same_half = jnp.where(same, 1.0, 0.0).astype(BF16) > 0
-    pair_half = jnp.where(row // 64 == col // 64, 1.0, 0.0).astype(BF16) > 0
+    same = row // BLOCK == col // BLOCK
+    same_pair = row // (2 * BLOCK) == col // (2 * BLOCK)
+    same_mask = jnp.where(same, 1.0, 0.0).astype(BF16) > 0
+    pair_mask = jnp.where(same_pair, 1.0, 0.0).astype(BF16) > 0
     zero = jnp.zeros((N, N), BF16)
+    small_row, small_col = iotas(BLOCK)
+    eye = jnp.where(small_row == small_col % BLOCK, 1.0, 0.0).astype(F32)
+    odd = (small_col // BLOCK) % 2 == 1
 
     def packed(matrix):
         return (matrix[0:32] + matrix[32:64]) + (matrix[64:96] + matrix[96:128])
@@ -87,38 +105,49 @@
         return [jnp.where(mask, jnp.concatenate([part] * copies, axis=0), zero) for part in parts]
 
     def stacked(parts, others):
-        return [jnp.concatenate([part, other], axis=0) for part, other in zip(parts, others)]
-
-    small_row, small_col = iotas(BLOCK)
-    eye = jnp.where(small_row == small_col % BLOCK, 1.0, 0.0).astype(F32)
-    power = packed(strict)
-    product = eye + power
-    parts = split3(power)
-    power = mm_parts(parts, spread(parts, same_half, 4))
+        return [jnp.concatenate(pair, axis=0) for pair in zip(parts, others)]
+
+    def linked(parts, corners, mask, copies):
+        left = [mm_parts(part, split3(corner)) for part, corner in zip(parts, corners)]
+        return [mm_parts(split3(value), spread(part, mask, copies)) for value, part in zip(left, parts)]
+
+    diags = [jnp.where(on_diag, tri, 0.0) for tri in triangles]
+    diag_cols = [jnp.sum(diag, axis=1, keepdims=True) for diag in diags]
+    diag_rows = [jnp.sum(diag, axis=0, keepdims=True) for diag in diags]
+    powers = [
+        packed(jnp.where(same & (row < col), -tri, 0.0) / diag) for tri, diag in zip(triangles, diag_cols)
+    ]
+    products = [eye + power for power in powers]
+    parts = [split3(power) for power in powers]
+    powers = [mm_parts(part, spread(part, same_mask, 4)) for part in parts]
     for _ in range(3):
-        parts = split3(power)
-        both = mm_parts(stacked(parts, split3(product)), spread(parts, same_half, 4))
-        product = product + both[BLOCK:]
-        power = both[:BLOCK]
-    parts = split3(power)
-    product = product + mm_parts(split3(product), spread(parts, same_half, 4))
-    inverse = product / diag_row
-    parts = split3(inverse)
-    corner = jnp.where((row // 64 == col // 64) & (row // 32 < col // 32), triangle, 0.0)
-    linked = mm_parts(split3(mm_parts(parts, split3(corner))), spread(parts, same_half, 4))
-    odd = (small_col // BLOCK) % 2 == 1
-    top = jnp.where(odd, -linked, inverse)
-    bottom = jnp.where(odd, inverse, 0.0)
-    pair = jnp.concatenate([top, bottom], axis=0)
-    pair_inverse = jnp.where(row // 64 == col // 64, jnp.concatenate([pair, pair], axis=0), 0.0)
-    parts = split3(pair)
-    corner = jnp.where(row // 64 < col // 64, triangle, 0.0)
-    linked = mm_parts(split3(mm_parts(parts, split3(corner))), spread(parts, pair_half, 2))
-    upper = pair_inverse[:64] - linked
-    return jnp.concatenate([upper, pair_inverse[64:]], axis=0)
-
-
-def leaf_kernel(q_hbm, g_hbm, blocks_hbm, sums_ref, send_ref, q_ref, g_ref, blocks_ref, sems):
+        parts = [split3(power) for power in powers]
+        both = [
+            mm_parts(stacked(part, split3(product)), spread(part, same_mask, 4))
+            for part, product in zip(parts, products)
+        ]
+        products = [product + value[BLOCK:] for product, value in zip(products, both)]
+        powers = [value[:BLOCK] for value in both]
+    parts = [split3(power) for power in powers]
+    products = [
+        product + mm_parts(split3(product), spread(part, same_mask, 4))
+        for product, part in zip(products, parts)
+    ]
+    inverses = [product / diag for product, diag in zip(products, diag_rows)]
+
+    corners = [jnp.where(same_pair & (row // BLOCK < col // BLOCK), tri, 0.0) for tri in triangles]
+    links = linked([split3(inverse) for inverse in inverses], corners, same_mask, 4)
+    pairs = [
+        jnp.concatenate([jnp.where(odd, -link, inverse), jnp.where(odd, inverse, 0.0)], axis=0)
+        for link, inverse in zip(links, inverses)
+    ]
+    corners = [jnp.where(row // (2 * BLOCK) < col // (2 * BLOCK), tri, 0.0) for tri in triangles]
+    links = linked([split3(pair) for pair in pairs], corners, pair_mask, 2)
+    wide = [jnp.where(same_pair, jnp.concatenate([pair, pair], axis=0), 0.0) for pair in pairs]
+    return [jnp.concatenate([full[:64] - link, full[64:]], axis=0) for full, link in zip(wide, links)]
+
+
+def leaf_kernel(after_ref, q_hbm, g_hbm, blocks_hbm, sums_ref, send_ref, q_ref, g_ref, blocks_ref, sems):
     copies = [
         pltpu.make_async_copy(g_hbm, g_ref, sems.at[0]),
         pltpu.make_async_copy(q_hbm, q_ref, sems.at[1]),
@@ -138,7 +167,7 @@
         send_ref[y, PIECE : 2 * PIECE] = second_t[y * PIECE : (y + 1) * PIECE]
 
 
-def near_kernel(z_ref, recv_ref, blocks_ref, after_ref, kept_ref, send_ref):
+def near_kernel(z_ref, recv_ref, blocks_ref, kept_ref, send_ref):
     z = z_ref[0]
     halves = [sum(recv_ref[4 * h + k, 0:PIECE] for k in range(4)) for h in range(2)]
     kept_ref[0] = halves[0]
@@ -182,31 +211,26 @@
         send_ref[y, 4 * PIECE : 5 * PIECE] = fifth
 
 
-def low_inverse_kernel(tri_ref, tris_ref, after_ref, out_ref):
-    out_ref[0] = tri_inverse(tri_ref[...])
-    for level in range(2):
-        out_ref[level + 1] = tri_inverse(tris_ref[level].astype(F32))
-
-
-def high_inverse_kernel(tris_ref, after_ref, out_ref):
-    for level in range(3):
-        out_ref[level] = tri_inverse(tris_ref[level + 2].astype(F32))
-
-
-def chain_kernel(tri_ref, g_ref, blocks_ref, tris_ref, root_ref, low_ref, high_ref, link_ref, gain_ref, base_ref, top_ref):
+def inverse_kernel(tri_ref, tris_ref, after_ref, out_ref):
+    tris = [tri_ref[...]] + [tris_ref[level].astype(F32) for level in range(LEVELS)]
+    for level, inverse in enumerate(tri_inverses(tris)):
+        out_ref[level] = inverse
+
+
+def chain_kernel(tri_ref, g_ref, blocks_ref, tris_ref, root_ref, inverse_ref, link_ref, gain_ref, base_ref, top_ref):
     tris = [tri_ref[...]] + [tris_ref[level].astype(F32) for level in range(LEVELS)]
     paths = [None] * (LEVELS + 1)
     paths[LEVELS - 1] = blocks_ref[LEVELS - 1].astype(F32)
     for level in reversed(range(LEVELS - 1)):
         paths[level] = mm(blocks_ref[level].astype(F32), paths[level + 1])
     for level in reversed(range(LEVELS)):
-        link = mm(tris[level], low_ref[level + 1] if level < 2 else high_ref[level - 2])
+        link = mm(tris[level], inverse_ref[level + 1])
         link_ref[level] = link
         if level == LEVELS - 1:
             gain_ref[level] = link - paths[level]
         else:
             gain_ref[level] = mm(link, paths[level + 1]) - paths[level]
-    base_ref[...] = mm(g_ref[...], mm(low_ref[0], paths[0]), NT)
+    base_ref[...] = mm(g_ref[...], mm(inverse_ref[0], paths[0]), NT)
     top_ref[...] = mm(tris[LEVELS], root_ref[...], NT)
 
 
@@ -215,14 +239,16 @@
     return jnp.concatenate(pieces, axis=0)
 
 
-def descend_kernel(recv_ref, sums_ref, q_ref, blocks_ref, link_ref, gain_ref, low_ref, base_ref, top_ref, out_ref):
+def descend_kernel(
+    recv_ref, sums_ref, q_ref, blocks_ref, link_ref, gain_ref, inverse_ref, base_ref, top_ref, out_ref
+):
     middle = top_ref[...] - gathered(recv_ref, LEVELS - 1)
     for level in reversed(range(LEVELS)):
         own = gathered(recv_ref, level - 1) if level else sums_ref[...]
-        spread = mm(link_ref[level], mirror_lower(middle))
-        middle = mm(gain_ref[level], own) + mm_exact(spread, blocks_ref[level], NT)
-    inner = mm(q_ref[...], mirror_lower(middle))
-    out_ref[...] = base_ref[...] + mm(inner, low_ref[0], NT)
+        spread = mm_short(link_ref[level], mirror_lower(middle))
+        middle = mm_short(gain_ref[level], own) + mm_exact_short(spread, blocks_ref[level], NT)
+    last = mm_short(mirror_lower(middle), inverse_ref[0], NT)
+    out_ref[...] = base_ref[...] + mm_short(q_ref[...], last)
 
 
 def kept(*shape):
@@ -263,24 +289,23 @@
         pltpu.SemaphoreType.DMA((3,)),
     )
     sums, send = call(
-        leaf_kernel, (kept(N, N), kept(N_Y, 2 * PIECE, N)), [PLAIN] * 3, "leaf", scratch
-    )(far_away(leaf_q), far_away(q_cot), far_away(node_blocks))
+        leaf_kernel, (kept(N, N), kept(N_Y, 2 * PIECE, N)), [SMEM] + [PLAIN] * 3, "leaf", scratch
+    )(z, far_away(leaf_q), far_away(q_cot), far_away(node_blocks))
     sums = near(sums)
     blocks, tris = near(node_blocks), near(node_tri)
     tri, cot, root, rows = near(leaf_tri), near(q_cot), near(root_cot), near(leaf_q)
 
     recv = near(lax.all_to_all(send, "y", 0, 0))
-    low = near(call(low_inverse_kernel, kept(3, N, N), [VMEM] * 3, "low")(tri, tris, sums))
     halves, send = call(
-        near_kernel, (kept(2, PIECE, N), kept(N_Z, PIECE, N)), [SMEM] + [VMEM] * 3, "near"
-    )(z, recv, blocks, low)
+        near_kernel, (kept(2, PIECE, N), kept(N_Z, PIECE, N)), [SMEM] + [VMEM] * 2, "near"
+    )(z, recv, blocks)
     halves = near(halves)
 
     recv = near(lax.all_to_all(send, "z", 0, 0))
-    high = near(call(high_inverse_kernel, kept(3, N, N), [VMEM] * 2, "high")(tris, halves))
+    inverses = near(call(inverse_kernel, kept(LEVELS + 1, N, N), [VMEM] * 3, "inverse")(tri, tris, halves))
     link, gain, base, top = call(
-        chain_kernel, (kept(LEVELS, N, N), kept(LEVELS, N, N), kept(ROWS, N), kept(N, N)), [VMEM] * 7, "chain"
-    )(tri, cot, blocks, tris, root, low, high)
+        chain_kernel, (kept(LEVELS, N, N), kept(LEVELS, N, N), kept(ROWS, N), kept(N, N)), [VMEM] * 6, "chain"
+    )(tri, cot, blocks, tris, root, inverses)
     link, gain, base, top = near(link), near(gain), near(base), near(top)
     mine, send = call(
         far_kernel, (kept(3, PIECE, N), kept(N_OUTER, PIECE, N)), [SMEM] + [VMEM] * 3, "far"
@@ -292,7 +317,7 @@
 
     recv = near(lax.all_to_all(send, "y", 0, 0))
     return call(descend_kernel, jax.ShapeDtypeStruct((ROWS, N), F32), [VMEM] * 9, "descend")(
-        recv, sums, rows, blocks, link, gain, low, base, top
+        recv, sums, rows, blocks, link, gain, inverses, base, top
     )
 
 

time: 81.4 us -> 80.3 us (0.986)
  blocking collectives: 27.4 us -> 43.6 us
  Pallas kernels: 17.2 us -> 9.44 us
  starting transfers between devices: 26.2 us -> 18.5 us
  waiting for transfers between devices: 9.93 us -> 8.27 us
    all_to_all x1 -> x2, blocking collectives: 14.4 us -> 30.6 us  [on_device(): recv = near(lax.all_to_all(send, 'y', 0, 0))]
    all_to_all x1 -> x0, starting transfers between devices: 7.79 us -> none  [on_device(): recv = near(lax.all_to_all(send, 'y', 0, 0))]
    pallas_call x3 -> x2, Pallas kernels: 10.5 us -> 3.54 us  [the longest x1 1.91 us: on_device(): call(inverse_kernel, kept(LEVELS + 1, N, N), [VMEM] * 3, 'inverse')]
    all_to_all x1 -> x0, waiting for transfers between devices: 3.82 us -> none  [on_device(): recv = near(lax.all_to_all(send, 'y', 0, 0))]
    all_to_all x1, waiting for transfers between devices: 6.11 us -> 8.27 us  [on_device(): recv = near(lax.all_to_all(send, 'z', 0, 0))]
    pallas_call x1, Pallas kernels: 3.7 us -> 2.83 us  [on_device(): call(descend_kernel, jax.ShapeDtypeStruct((ROWS, N), F32), [VMEM] * 9, 'd...]
  transfers between devices with their start and end apart: 2 -> 1, of which waited for: 2 -> 1; matrix products, arithmetic and copies ran while one was open for 0% -> 0% of each run, Pallas kernels for 12% -> 5%
where the time goes in v4:
time: 80.3 us; the launch traced here: 79.9 us
  blocking collectives  43.6 us (54%)
  starting transfers between devices  18.5 us (23%)
  Pallas kernels  9.44 us (12%)
  waiting for transfers between devices  8.27 us (10%)
    all_to_all x2, blocking collectives, on_device(): recv = near(lax.all_to_all(send, 'y', 0, 0))  30.6 us
    all_to_all x1, starting transfers between devices, on_device(): recv = near(lax.all_to_all(send, 'z', 0, 0))  18.5 us
    all_to_all x1, blocking collectives, on_device(): recv = near(lax.all_to_all(send, 'outer', 0, 0))  12.9 us
    all_to_all x1, waiting for transfers between devices, on_device(): recv = near(lax.all_to_all(send, 'z', 0, 0))  8.27 us
    pallas_call x1, Pallas kernels, on_device(): call(descend_kernel, jax.ShapeDtypeStruct((ROWS, N), F32), [VMEM] * 9, 'd...  2.83 us
    pallas_call x1, Pallas kernels, on_device(): call(inverse_kernel, kept(LEVELS + 1, N, N), [VMEM] * 3, 'inverse')  1.91 us
    pallas_call x1, Pallas kernels, on_device(): call(chain_kernel, (kept(LEVELS, N, N), kept(LEVELS, N, N), kept(ROWS, N)...  1.72 us
    pallas_call x1, Pallas kernels, on_device(): call(leaf_kernel, (kept(N, N), kept(N_Y, 2 * PIECE, N)), [SMEM] + [PLAIN]...  1.63 us
  transfers between devices with their start and end apart: 1, of which 1 were waited for; matrix products, arithmetic and copies ran while one was open for 0% of the time, Pallas kernels for 5%

profile of v4, /device:TPU:1, one launch (start us, length us, event | category | flops | bytes accessed | tf_op | source)
XLA Modules:
  0.0 79.9 jit_solution(14422934582521426545)
XLA Ops:
  0.0 1.6 %leaf.1 = (f32[128,128]{1,0:T(8,128)S(1)}, f32[8,32,128]{2,1,0:T(8,128)S(1)}) custom-call(s32[1]{0:T(128)} %bitcast.after_ref.z_ref, f32[256,128]{1,0:T(8,128)} %q_ref.1, f32[256,128]{1,0:T(8,128)} %g_ref.1, bf16[5,128,128]{2,1,0:T(8,128)(2,1)} %blocks_ref.7), custom_call_target="tpu_custom_call" | custom-call | tf_op jit(solution)/shard_map/leaf/pallas_call | solution.py:291
  1.6 0.0 copy-start
  1.6 15.5 %all_to_all.20.recv_ref = f32[8,32,128]{2,1,0:T(8,128)S(1)} all-to-all(f32[8,32,128]{2,1,0:T(8,128)S(1)} %get-tuple-element.15), channel_id=1, replica_groups=mesh['outer'=8,'z'=16,'y'=8] {'y'}, dimensions={0} | all-to-all | bytes 262144 | tf_op jit(solution)/shard_map/all_to_all | solution.py:298
  17.1 0.0 copy-done
  17.2 0.9 %near.1 = (f32[2,16,128]{2,1,0:T(8,128)S(1)}, f32[16,16,128]{2,1,0:T(8,128)}) custom-call(s32[1]{0:T(128)} %bitcast.after_ref.z_ref, f32[8,32,128]{2,1,0:T(8,128)S(1)} %all_to_all.20.recv_ref, bf16[5,128,128]{2,1,0:T(8,128)(2,1)S(1)} %copy-done), custom_call_target="tpu_custom_call" | custom-call | tf_op jit(solution)/shard_map/near/pallas_call | solution.py:299
  18.1 0.0 copy-start.1
  18.1 0.0 copy-start.4
  18.1 18.5 %all-to-all-start.1 = ((f32[16,16,128]{2,1,0:T(8,128)}), f32[16,16,128]{2,1,0:T(8,128)S(1)}, u32[]{:S(2)}, u32[]{:S(2)}) async-start(f32[16,16,128]{2,1,0:T(8,128)} %get-tuple-element.16), calls=%async_computation.1 | async-start | bytes 262144 | tf_op jit(solution)/shard_map/all_to_all | solution.py:304
  36.6 0.0 copy-done.1
  36.7 0.0 copy-done.4
  36.7 0.0 copy-start.2
  36.7 0.0 copy-start.5
  36.7 1.9 %inverse.1.inverse_ref = f32[6,128,128]{2,1,0:T(8,128)S(1)} custom-call(f32[128,128]{1,0:T(8,128)S(1)} %copy-done.4, bf16[5,128,128]{2,1,0:T(8,128)(2,1)S(1)} %copy-done.1, f32[2,16,128]{2,1,0:T(8,128)S(1)} %get-tuple-element.17.after_ref.halves_ref), custom_call_target="tpu_custom_call" | custom-call | tf_op jit(solution)/shard_map/inverse/pallas_call | solution.py:305
  38.6 0.0 copy-done.2
  38.6 0.0 copy-done.5
  38.6 1.7 %chain.1 = (f32[5,128,128]{2,1,0:T(8,128)S(1)}, f32[5,128,128]{2,1,0:T(8,128)S(1)}, f32[256,128]{1,0:T(8,128)S(1)}, f32[128,128]{1,0:T(8,128)S(1)}) custom-call(f32[128,128]{1,0:T(8,128)S(1)} %copy-done.4, f32[256,128]{1,0:T(8,128)S(1)} %copy-done.2, bf16[5,128,128]{2,1,0:T(8,128)(2,1)S(1)} %copy-done, bf16[5,128,128]{2,1,0:T(8,128)(2,1)S(1)} %copy-done.1, ...), custom_call_target="tpu_custom_call" | custom-call | tf_op jit(solution)/shard_map/chain/pallas_call | solution.py:306
  40.4 8.3 %all-to-all-done.1.recv_ref = f32[16,16,128]{2,1,0:T(8,128)S(1)} async-done(((f32[16,16,128]{2,1,0:T(8,128)}), f32[16,16,128]{2,1,0:T(8,128)S(1)}, u32[]{:S(2)}, u32[]{:S(2)}) %all-to-all-start.1) | async-done | bytes 131104 | tf_op jit(solution)/shard_map/all_to_all | solution.py:304
  48.6 0.4 far.1
  49.0 12.9 %all_to_all.21.recv_ref = f32[8,16,128]{2,1,0:T(8,128)S(1)} all-to-all(f32[8,16,128]{2,1,0:T(8,128)S(1)} %get-tuple-element.19), channel_id=1, replica_groups=mesh['outer'=8,'z'=16,'y'=8] {'outer'}, dimensions={0} | all-to-all | bytes 131072 | tf_op jit(solution)/shard_map/all_to_all | solution.py:315
  61.9 0.0 copy-start.3
  62.0 15.2 %all_to_all.22.recv_ref = f32[8,80,128]{2,1,0:T(8,128)S(1)} all-to-all(f32[8,80,128]{2,1,0:T(8,128)S(1)} %join.1), channel_id=1, replica_groups=mesh['outer'=8,'z'=16,'y'=8] {'y'}, dimensions={0} | all-to-all | bytes 655360 | tf_op jit(solution)/shard_map/all_to_all | solution.py:318
  77.1 0.0 copy-done.3
  77.1 2.8 %descend.1 = f32[256,128]{1,0:T(8,128)} custom-call(f32[8,80,128]{2,1,0:T(8,128)S(1)} %all_to_all.22.recv_ref, f32[128,128]{1,0:T(8,128)S(1)} %get-tuple-element.21.sums_ref, f32[256,128]{1,0:T(8,128)S(1)} %copy-done.3, bf16[5,128,128]{2,1,0:T(8,128)(2,1)S(1)} %copy-done, f32[5,128,128]{2,1,0:T(8,128)S(1)} %get-tuple-element.22.link_ref, ...), custom_call_target="tpu_custom_call" | custom-call | tf_op jit(solution)/shard_map/descend/pallas_call | solution.py:319
  (1 shorter events, 0.0 us)
Async XLA Ops:
  1.6 15.5 %copy-start = (bf16[5,128,128]{2,1,0:T(8,128)(2,1)S(1)}, bf16[5,128,128]{2,1,0:T(8,128)(2,1)}, u32[]{:S(2)}) copy-start(bf16[5,128,128]{2,1,0:T(8,128)(2,1)} %blocks_ref.7) | copy-start | bytes 491524
  18.1 18.6 %copy-start.1 = (bf16[5,128,128]{2,1,0:T(8,128)(2,1)S(1)}, bf16[5,128,128]{2,1,0:T(8,128)(2,1)}, u32[]{:S(2)}) copy-start(bf16[5,128,128]{2,1,0:T(8,128)(2,1)} %tris_ref.3) | copy-start | bytes 491524
  18.1 18.6 %copy-start.4 = (f32[128,128]{1,0:T(8,128)S(1)}, f32[128,128]{1,0:T(8,128)}, u32[]{:S(2)}) copy-start(f32[128,128]{1,0:T(8,128)} %tri_ref.3) | copy-start | bytes 196612
  18.1 30.5 %all-to-all-start.1 = ((f32[16,16,128]{2,1,0:T(8,128)}), f32[16,16,128]{2,1,0:T(8,128)S(1)}, u32[]{:S(2)}, u32[]{:S(2)}) async-start(f32[16,16,128]{2,1,0:T(8,128)} %get-tuple-element.16), calls=%async_computation.1 | async-start | bytes 262144 | tf_op jit(solution)/shard_map/all_to_all | solution.py:304
  36.7 1.9 %copy-start.2 = (f32[256,128]{1,0:T(8,128)S(1)}, f32[256,128]{1,0:T(8,128)}, u32[]{:S(2)}) copy-start(f32[256,128]{1,0:T(8,128)} %g_ref.1) | copy-start | bytes 393220
  36.7 1.9 %copy-start.5 = (f32[128,128]{1,0:T(8,128)S(1)}, f32[128,128]{1,0:T(8,128)}, u32[]{:S(2)}) copy-start(f32[128,128]{1,0:T(8,128)} %root_ref.1) | copy-start | bytes 196612
  61.9 15.2 %copy-start.3 = (f32[256,128]{1,0:T(8,128)S(1)}, f32[256,128]{1,0:T(8,128)}, u32[]{:S(2)}) copy-start(f32[256,128]{1,0:T(8,128)} %q_ref.1) | copy-start | bytes 393220

commit v5 on v4

--- a/solution.py
+++ b/solution.py
@@ -7,11 +7,11 @@
 
 N = 128
 BLOCK = 32
-PIECE = 16
+PIECE = 8
 ROWS = 256
 LEVELS = 5
-N_Y = 8
-N_Z = 16
+N_NEAR = 16
+N_FAR = 8
 N_OUTER = 8
 
 F32 = jnp.float32
@@ -162,53 +162,48 @@
     copies[2].wait()
     first_t = mm_exact(sums_t, blocks_ref[0])
     second_t = mm_exact(first_t, blocks_ref[1])
-    for y in range(N_Y):
-        send_ref[y, 0:PIECE] = first_t[y * PIECE : (y + 1) * PIECE]
-        send_ref[y, PIECE : 2 * PIECE] = second_t[y * PIECE : (y + 1) * PIECE]
-
-
-def near_kernel(z_ref, recv_ref, blocks_ref, kept_ref, send_ref):
-    z = z_ref[0]
-    halves = [sum(recv_ref[4 * h + k, 0:PIECE] for k in range(4)) for h in range(2)]
-    kept_ref[0] = halves[0]
-    kept_ref[1] = halves[1]
-    second = sum(recv_ref[k, PIECE : 2 * PIECE] for k in range(N_Y))
+    for peer in range(N_NEAR):
+        send_ref[peer, 0:PIECE] = first_t[peer * PIECE : (peer + 1) * PIECE]
+        send_ref[peer, PIECE : 2 * PIECE] = second_t[peer * PIECE : (peer + 1) * PIECE]
+
+
+def near_kernel(place_ref, recv_ref, blocks_ref, kept_ref, send_ref):
+    place = place_ref[0]
+    for group in range(4):
+        kept_ref[group] = sum(recv_ref[4 * group + k, 0:PIECE] for k in range(4))
+    second = sum(recv_ref[k, PIECE : 2 * PIECE] for k in range(N_NEAR))
+    kept_ref[4] = second
     third = mm_exact(second, blocks_ref[2])
     fourth = mm_exact(third, blocks_ref[3])
-    for peer in range(N_Z):
-        same_pair = (z // 2) == (peer // 2)
-        same_octet = (z // 8) == (peer // 8)
-        send_ref[peer] = jnp.where(same_pair, second, jnp.where(same_octet, third, fourth))
-
-
-def far_kernel(z_ref, recv_ref, blocks_ref, after_ref, kept_ref, send_ref):
-    z = z_ref[0]
+    for peer in range(N_FAR):
+        send_ref[peer] = jnp.where(place // 4 == peer // 4, third, fourth)
+
+
+def far_kernel(place_ref, recv_ref, blocks_ref, after_ref, kept_ref, send_ref):
+    place = place_ref[0]
     zero = jnp.zeros((PIECE, N), F32)
-    second, third, fourth = zero, zero, zero
-    for peer in range(N_Z):
-        same_pair = (z // 2) == (peer // 2)
-        same_octet = (z // 8) == (peer // 8)
+    third, fourth = zero, zero
+    for peer in range(N_FAR):
+        same = place // 4 == peer // 4
         value = recv_ref[peer]
-        second = second + jnp.where(same_pair, value, zero)
-        third = third + jnp.where(same_octet & jnp.logical_not(same_pair), value, zero)
-        fourth = fourth + jnp.where(same_octet, zero, value)
-    third = third + mm_exact(second, blocks_ref[2])
+        third = third + jnp.where(same, value, zero)
+        fourth = fourth + jnp.where(same, zero, value)
     fourth = fourth + mm_exact(third, blocks_ref[3])
     fifth = mm_exact(fourth, blocks_ref[4])
-    kept_ref[0] = second
-    kept_ref[1] = third
-    kept_ref[2] = fourth
+    kept_ref[0] = third
+    kept_ref[1] = fourth
     for peer in range(N_OUTER):
         send_ref[peer] = fifth
 
 
-def join_kernel(recv_ref, halves_ref, kept_ref, send_ref):
+def join_kernel(recv_ref, sums_ref, kept_ref, send_ref):
     fifth = sum(recv_ref[k] for k in range(N_OUTER))
-    for y in range(N_Y):
-        send_ref[y, 0:PIECE] = halves_ref[y // 4]
-        for level in range(3):
-            send_ref[y, (level + 1) * PIECE : (level + 2) * PIECE] = kept_ref[level]
-        send_ref[y, 4 * PIECE : 5 * PIECE] = fifth
+    for peer in range(N_NEAR):
+        send_ref[peer, 0:PIECE] = sums_ref[peer // 4]
+        send_ref[peer, PIECE : 2 * PIECE] = sums_ref[4]
+        send_ref[peer, 2 * PIECE : 3 * PIECE] = kept_ref[0]
+        send_ref[peer, 3 * PIECE : 4 * PIECE] = kept_ref[1]
+        send_ref[peer, 4 * PIECE : 5 * PIECE] = fifth
 
 
 def inverse_kernel(tri_ref, tris_ref, after_ref, out_ref):
@@ -235,7 +230,7 @@
 
 
 def gathered(recv_ref, slot):
-    pieces = [recv_ref[y, slot * PIECE : (slot + 1) * PIECE] for y in range(N_Y)]
+    pieces = [recv_ref[peer, slot * PIECE : (slot + 1) * PIECE] for peer in range(N_NEAR)]
     return jnp.concatenate(pieces, axis=0)
 
 
@@ -281,7 +276,7 @@
 
 
 def on_device(leaf_q, q_cot, leaf_tri, node_blocks, node_tri, root_cot):
-    z = lax.axis_index("z").astype(jnp.int32).reshape(1)
+    place = lax.axis_index("far").astype(jnp.int32).reshape(1)
     scratch = (
         kept(ROWS, N),
         kept(ROWS, N),
@@ -289,41 +284,41 @@
         pltpu.SemaphoreType.DMA((3,)),
     )
     sums, send = call(
-        leaf_kernel, (kept(N, N), kept(N_Y, 2 * PIECE, N)), [SMEM] + [PLAIN] * 3, "leaf", scratch
-    )(z, far_away(leaf_q), far_away(q_cot), far_away(node_blocks))
+        leaf_kernel, (kept(N, N), kept(N_NEAR, 2 * PIECE, N)), [SMEM] + [PLAIN] * 3, "leaf", scratch
+    )(place, far_away(leaf_q), far_away(q_cot), far_away(node_blocks))
     sums = near(sums)
     blocks, tris = near(node_blocks), near(node_tri)
     tri, cot, root, rows = near(leaf_tri), near(q_cot), near(root_cot), near(leaf_q)
 
-    recv = near(lax.all_to_all(send, "y", 0, 0))
-    halves, send = call(
-        near_kernel, (kept(2, PIECE, N), kept(N_Z, PIECE, N)), [SMEM] + [VMEM] * 2, "near"
-    )(z, recv, blocks)
-    halves = near(halves)
-
-    recv = near(lax.all_to_all(send, "z", 0, 0))
-    inverses = near(call(inverse_kernel, kept(LEVELS + 1, N, N), [VMEM] * 3, "inverse")(tri, tris, halves))
+    recv = near(lax.all_to_all(send, "near", 0, 0))
+    low, send = call(
+        near_kernel, (kept(5, PIECE, N), kept(N_FAR, PIECE, N)), [SMEM] + [VMEM] * 2, "near"
+    )(place, recv, blocks)
+    low = near(low)
+
+    recv = near(lax.all_to_all(send, "far", 0, 0))
+    inverses = near(call(inverse_kernel, kept(LEVELS + 1, N, N), [VMEM] * 3, "inverse")(tri, tris, low))
     link, gain, base, top = call(
         chain_kernel, (kept(LEVELS, N, N), kept(LEVELS, N, N), kept(ROWS, N), kept(N, N)), [VMEM] * 6, "chain"
     )(tri, cot, blocks, tris, root, inverses)
     link, gain, base, top = near(link), near(gain), near(base), near(top)
-    mine, send = call(
-        far_kernel, (kept(3, PIECE, N), kept(N_OUTER, PIECE, N)), [SMEM] + [VMEM] * 3, "far"
-    )(z, recv, blocks, top)
-    mine = near(mine)
+    high, send = call(
+        far_kernel, (kept(2, PIECE, N), kept(N_OUTER, PIECE, N)), [SMEM] + [VMEM] * 3, "far"
+    )(place, recv, blocks, top)
+    high = near(high)
 
     recv = near(lax.all_to_all(send, "outer", 0, 0))
-    send = call(join_kernel, kept(N_Y, 5 * PIECE, N), [VMEM] * 3, "join")(recv, halves, mine)
-
-    recv = near(lax.all_to_all(send, "y", 0, 0))
+    send = call(join_kernel, kept(N_NEAR, 5 * PIECE, N), [VMEM] * 3, "join")(recv, low, high)
+
+    recv = near(lax.all_to_all(send, "near", 0, 0))
     return call(descend_kernel, jax.ShapeDtypeStruct((ROWS, N), F32), [VMEM] * 9, "descend")(
         recv, sums, rows, blocks, link, gain, inverses, base, top
     )
 
 
 def solution(mesh):
-    split = Mesh(mesh.devices.reshape(N_OUTER, N_Z, N_Y), ("outer", "z", "y"))
-    every = ("outer", "z", "y")
+    every = ("outer", "far", "near")
+    split = Mesh(mesh.devices.reshape(N_OUTER, N_FAR, N_NEAR), every)
     return jax.shard_map(
         on_device,
         mesh=split,

time: 80.3 us -> 78.8 us (0.981)
  the two profiles are of different devices: /device:TPU:1 before, /device:TPU:8 now
where the time goes in v5:
time: 78.8 us; the launch traced here: 78.5 us
  blocking collectives  48.2 us (61%)
  starting transfers between devices  11.6 us (15%)
  waiting for transfers between devices  9.29 us (12%)
  Pallas kernels  9.27 us (12%)
    all_to_all x2, blocking collectives, on_device(): recv = near(lax.all_to_all(send, 'near', 0, 0))  38.7 us
    all_to_all x1, starting transfers between devices, on_device(): recv = near(lax.all_to_all(send, 'far', 0, 0))  11.6 us
    all_to_all x1, blocking collectives, on_device(): recv = near(lax.all_to_all(send, 'outer', 0, 0))  9.54 us
    all_to_all x1, waiting for transfers between devices, on_device(): recv = near(lax.all_to_all(send, 'far', 0, 0))  9.29 us
    pallas_call x1, Pallas kernels, on_device(): call(descend_kernel, jax.ShapeDtypeStruct((ROWS, N), F32), [VMEM] * 9, 'd...  2.84 us
    pallas_call x1, Pallas kernels, on_device(): call(inverse_kernel, kept(LEVELS + 1, N, N), [VMEM] * 3, 'inverse')  1.9 us
    pallas_call x1, Pallas kernels, on_device(): call(chain_kernel, (kept(LEVELS, N, N), kept(LEVELS, N, N), kept(ROWS, N)...  1.72 us
    pallas_call x1, Pallas kernels, on_device(): call(leaf_kernel, (kept(N, N), kept(N_NEAR, 2 * PIECE, N)), [SMEM] + [PLA...  1.63 us
  transfers between devices with their start and end apart: 1, of which 1 were waited for; matrix products, arithmetic and copies ran while one was open for 0% of the time, Pallas kernels for 5%

profile of v5, /device:TPU:8, one launch (start us, length us, event | category | flops | bytes accessed | tf_op | source)
XLA Modules:
  0.0 78.5 jit_solution(15088620082367474257)
XLA Ops:
  0.0 1.6 %leaf.1 = (f32[128,128]{1,0:T(8,128)S(1)}, f32[16,16,128]{2,1,0:T(8,128)S(1)}) custom-call(s32[1]{0:T(128)} %bitcast.after_ref.place_ref, f32[256,128]{1,0:T(8,128)} %q_ref.1, f32[256,128]{1,0:T(8,128)} %g_ref.1, bf16[5,128,128]{2,1,0:T(8,128)(2,1)} %blocks_ref.7), custom_call_target="tpu_custom_call" | custom-call | tf_op jit(solution)/shard_map/leaf/pallas_call | solution.py:286
  1.6 0.0 copy-start
  1.6 23.3 %all_to_all.20.recv_ref = f32[16,16,128]{2,1,0:T(8,128)S(1)} all-to-all(f32[16,16,128]{2,1,0:T(8,128)S(1)} %get-tuple-element.15), channel_id=1, replica_groups=mesh['outer'=8,'far'=8,'near'=16] {'near'}, dimensions={0} | all-to-all | bytes 262144 | tf_op jit(solution)/shard_map/all_to_all | solution.py:293
  25.0 0.0 copy-done
  25.0 0.0 copy-start.1
  25.0 0.9 %near.1 = (f32[5,8,128]{2,1,0:T(8,128)S(1)}, f32[8,8,128]{2,1,0:T(8,128)}) custom-call(s32[1]{0:T(128)} %bitcast.after_ref.place_ref, f32[16,16,128]{2,1,0:T(8,128)S(1)} %all_to_all.20.recv_ref, bf16[5,128,128]{2,1,0:T(8,128)(2,1)S(1)} %copy-done), custom_call_target="tpu_custom_call" | custom-call | tf_op jit(solution)/shard_map/near/pallas_call | solution.py:294
  25.9 0.0 copy-start.4
  25.9 11.6 %all-to-all-start.1 = ((f32[8,8,128]{2,1,0:T(8,128)}), f32[8,8,128]{2,1,0:T(8,128)S(1)}, u32[]{:S(2)}, u32[]{:S(2)}) async-start(f32[8,8,128]{2,1,0:T(8,128)} %get-tuple-element.16), calls=%async_computation.1 | async-start | bytes 65536 | tf_op jit(solution)/shard_map/all_to_all | solution.py:299
  37.5 0.0 copy-done.1
  37.5 0.0 copy-done.4
  37.5 0.0 copy-start.2
  37.5 0.0 copy-start.5
  37.5 1.9 %inverse.1.inverse_ref = f32[6,128,128]{2,1,0:T(8,128)S(1)} custom-call(f32[128,128]{1,0:T(8,128)S(1)} %copy-done.4, bf16[5,128,128]{2,1,0:T(8,128)(2,1)S(1)} %copy-done.1, f32[5,8,128]{2,1,0:T(8,128)S(1)} %get-tuple-element.17.after_ref.sums_ref), custom_call_target="tpu_custom_call" | custom-call | tf_op jit(solution)/shard_map/inverse/pallas_call | solution.py:300
  39.4 0.0 copy-done.2
  39.4 0.0 copy-done.5
  39.4 1.7 %chain.1 = (f32[5,128,128]{2,1,0:T(8,128)S(1)}, f32[5,128,128]{2,1,0:T(8,128)S(1)}, f32[256,128]{1,0:T(8,128)S(1)}, f32[128,128]{1,0:T(8,128)S(1)}) custom-call(f32[128,128]{1,0:T(8,128)S(1)} %copy-done.4, f32[256,128]{1,0:T(8,128)S(1)} %copy-done.2, bf16[5,128,128]{2,1,0:T(8,128)(2,1)S(1)} %copy-done, bf16[5,128,128]{2,1,0:T(8,128)(2,1)S(1)} %copy-done.1, ...), custom_call_target="tpu_custom_call" | custom-call | tf_op jit(solution)/shard_map/chain/pallas_call | solution.py:301
  41.2 9.3 %all-to-all-done.1.recv_ref = f32[8,8,128]{2,1,0:T(8,128)S(1)} async-done(((f32[8,8,128]{2,1,0:T(8,128)}), f32[8,8,128]{2,1,0:T(8,128)S(1)}, u32[]{:S(2)}, u32[]{:S(2)}) %all-to-all-start.1) | async-done | bytes 32800 | tf_op jit(solution)/shard_map/all_to_all | solution.py:299
  50.5 0.3 far.1
  50.7 9.5 %all_to_all.21.recv_ref = f32[8,8,128]{2,1,0:T(8,128)S(1)} all-to-all(f32[8,8,128]{2,1,0:T(8,128)S(1)} %get-tuple-element.19), channel_id=1, replica_groups=mesh['outer'=8,'far'=8,'near'=16] {'outer'}, dimensions={0} | all-to-all | bytes 65536 | tf_op jit(solution)/shard_map/all_to_all | solution.py:310
  60.3 0.0 copy-start.3
  60.3 15.4 %all_to_all.22.recv_ref = f32[16,40,128]{2,1,0:T(8,128)S(1)} all-to-all(f32[16,40,128]{2,1,0:T(8,128)S(1)} %join.1), channel_id=1, replica_groups=mesh['outer'=8,'far'=8,'near'=16] {'near'}, dimensions={0} | all-to-all | bytes 655360 | tf_op jit(solution)/shard_map/all_to_all | solution.py:313
  75.7 0.0 copy-done.3
  75.7 2.8 %descend.1 = f32[256,128]{1,0:T(8,128)} custom-call(f32[16,40,128]{2,1,0:T(8,128)S(1)} %all_to_all.22.recv_ref, f32[128,128]{1,0:T(8,128)S(1)} %get-tuple-element.21.sums_ref, f32[256,128]{1,0:T(8,128)S(1)} %copy-done.3, bf16[5,128,128]{2,1,0:T(8,128)(2,1)S(1)} %copy-done, f32[5,128,128]{2,1,0:T(8,128)S(1)} %get-tuple-element.22.link_ref, ...), custom_call_target="tpu_custom_call" | custom-call | tf_op jit(solution)/shard_map/descend/pallas_call | solution.py:314
  (1 shorter events, 0.0 us)
Async XLA Ops:
  1.6 23.3 %copy-start = (bf16[5,128,128]{2,1,0:T(8,128)(2,1)S(1)}, bf16[5,128,128]{2,1,0:T(8,128)(2,1)}, u32[]{:S(2)}) copy-start(bf16[5,128,128]{2,1,0:T(8,128)(2,1)} %blocks_ref.7) | copy-start | bytes 491524
  25.0 12.5 %copy-start.1 = (bf16[5,128,128]{2,1,0:T(8,128)(2,1)S(1)}, bf16[5,128,128]{2,1,0:T(8,128)(2,1)}, u32[]{:S(2)}) copy-start(bf16[5,128,128]{2,1,0:T(8,128)(2,1)} %tris_ref.3) | copy-start | bytes 491524
  25.9 11.6 %copy-start.4 = (f32[128,128]{1,0:T(8,128)S(1)}, f32[128,128]{1,0:T(8,128)}, u32[]{:S(2)}) copy-start(f32[128,128]{1,0:T(8,128)} %tri_ref.3) | copy-start | bytes 196612
  25.9 24.6 %all-to-all-start.1 = ((f32[8,8,128]{2,1,0:T(8,128)}), f32[8,8,128]{2,1,0:T(8,128)S(1)}, u32[]{:S(2)}, u32[]{:S(2)}) async-start(f32[8,8,128]{2,1,0:T(8,128)} %get-tuple-element.16), calls=%async_computation.1 | async-start | bytes 65536 | tf_op jit(solution)/shard_map/all_to_all | solution.py:299
  37.5 1.9 %copy-start.2 = (f32[256,128]{1,0:T(8,128)S(1)}, f32[256,128]{1,0:T(8,128)}, u32[]{:S(2)}) copy-start(f32[256,128]{1,0:T(8,128)} %g_ref.1) | copy-start | bytes 393220
  37.5 1.9 %copy-start.5 = (f32[128,128]{1,0:T(8,128)S(1)}, f32[128,128]{1,0:T(8,128)}, u32[]{:S(2)}) copy-start(f32[128,128]{1,0:T(8,128)} %root_ref.1) | copy-start | bytes 196612
  60.3 15.4 %copy-start.3 = (f32[256,128]{1,0:T(8,128)S(1)}, f32[256,128]{1,0:T(8,128)}, u32[]{:S(2)}) copy-start(f32[256,128]{1,0:T(8,128)} %q_ref.1) | copy-start | bytes 393220

commit v6 on v5

--- a/solution.py
+++ b/solution.py
@@ -49,11 +49,20 @@
     return mm_parts(split3(left), split3(right), dims)
 
 
+def mm_exact_parts(left, right, dims=NN):
+    rows = left[0].shape[0]
+    full = dot(jnp.concatenate(left, axis=0), right, dims)
+    return full[:rows] + (full[rows : 2 * rows] + full[2 * rows :])
+
+
 def mm_exact(left, right, dims=NN):
-    rows = left.shape[0]
-    lh, lm, ll = split3(left)
-    full = dot(jnp.concatenate([lh, lm, ll], axis=0), right, dims)
-    return full[:rows] + (full[rows : 2 * rows] + full[2 * rows :])
+    return mm_exact_parts(split3(left), right, dims)
+
+
+def mm_exact_left(left, right, dims=NN):
+    free = 1 - dims[1][0]
+    full = dot(left, jnp.concatenate(split3(right), axis=free), dims)
+    return full[:, :N] + (full[:, N : 2 * N] + full[:, 2 * N :])
 
 
 def split2(value):
@@ -108,7 +117,10 @@
         return [jnp.concatenate(pair, axis=0) for pair in zip(parts, others)]
 
     def linked(parts, corners, mask, copies):
-        left = [mm_parts(part, split3(corner)) for part, corner in zip(parts, corners)]
+        left = [mm_parts(part, split3(corner)) for part, corner in zip(parts[:1], corners[:1])]
+        left += [
+            mm_exact_parts(part, corner.astype(BF16)) for part, corner in zip(parts[1:], corners[1:])
+        ]
         return [mm_parts(split3(value), spread(part, mask, copies)) for value, part in zip(left, parts)]
 
     diags = [jnp.where(on_diag, tri, 0.0) for tri in triangles]
@@ -212,26 +224,40 @@
         out_ref[level] = inverse
 
 
-def chain_kernel(tri_ref, g_ref, blocks_ref, tris_ref, root_ref, inverse_ref, link_ref, gain_ref, base_ref, top_ref):
-    tris = [tri_ref[...]] + [tris_ref[level].astype(F32) for level in range(LEVELS)]
-    paths = [None] * (LEVELS + 1)
+def chain_kernel(
+    tri_ref, g_ref, blocks_ref, tris_ref, root_ref, inverse_ref, link_ref, gain_ref, base_ref, top_ref
+):
+    paths = [None] * LEVELS
     paths[LEVELS - 1] = blocks_ref[LEVELS - 1].astype(F32)
     for level in reversed(range(LEVELS - 1)):
-        paths[level] = mm(blocks_ref[level].astype(F32), paths[level + 1])
+        paths[level] = mm_exact_left(blocks_ref[level], paths[level + 1])
     for level in reversed(range(LEVELS)):
-        link = mm(tris[level], inverse_ref[level + 1])
+        if level:
+            link = mm_exact_left(tris_ref[level - 1], inverse_ref[level + 1])
+        else:
+            link = mm(tri_ref[...], inverse_ref[1])
         link_ref[level] = link
         if level == LEVELS - 1:
             gain_ref[level] = link - paths[level]
         else:
             gain_ref[level] = mm(link, paths[level + 1]) - paths[level]
     base_ref[...] = mm(g_ref[...], mm(inverse_ref[0], paths[0]), NT)
-    top_ref[...] = mm(tris[LEVELS], root_ref[...], NT)
+    top_ref[...] = mm_exact_left(tris_ref[LEVELS - 1], root_ref[...], NT)
 
 
 def gathered(recv_ref, slot):
     pieces = [recv_ref[peer, slot * PIECE : (slot + 1) * PIECE] for peer in range(N_NEAR)]
     return jnp.concatenate(pieces, axis=0)
+
+
+def mm_mirrored(left, lower):
+    row, col = iotas()
+    lh, ll = split2(left)
+    ah, al = split2(jnp.where(row >= col, lower, 0.0))
+    bh, bl = split2(jnp.where(row > col, lower, 0.0))
+    wide = jnp.concatenate([lh, ll, lh], axis=1)
+    direct = dot(wide, jnp.concatenate([ah, ah, al], axis=0), NN)
+    return direct + dot(wide, jnp.concatenate([bh, bh, bl], axis=1), NT)
 
 
 def descend_kernel(
@@ -240,7 +266,7 @@
     middle = top_ref[...] - gathered(recv_ref, LEVELS - 1)
     for level in reversed(range(LEVELS)):
         own = gathered(recv_ref, level - 1) if level else sums_ref[...]
-        spread = mm_short(link_ref[level], mirror_lower(middle))
+        spread = mm_mirrored(link_ref[level], middle)
         middle = mm_short(gain_ref[level], own) + mm_exact_short(spread, blocks_ref[level], NT)
     last = mm_short(mirror_lower(middle), inverse_ref[0], NT)
     out_ref[...] = base_ref[...] + mm_short(q_ref[...], last)

time: 78.8 us -> 78.7 us (level)
  transfers between devices with their start and end apart: 1 -> 1, of which waited for: 1 -> 1; matrix products, arithmetic and copies ran while one was open for 0% -> 0% of each run, Pallas kernels for 5% -> 4%
where the time goes in v6:
time: 78.7 us; the launch traced here: 78.4 us
  blocking collectives  48.2 us (61%)
  starting transfers between devices  11.6 us (15%)
  waiting for transfers between devices  9.61 us (12%)
  Pallas kernels  8.84 us (11%)
    all_to_all x2, blocking collectives, on_device(): recv = near(lax.all_to_all(send, 'near', 0, 0))  38.7 us
    all_to_all x1, starting transfers between devices, on_device(): recv = near(lax.all_to_all(send, 'far', 0, 0))  11.6 us
    all_to_all x1, waiting for transfers between devices, on_device(): recv = near(lax.all_to_all(send, 'far', 0, 0))  9.61 us
    all_to_all x1, blocking collectives, on_device(): recv = near(lax.all_to_all(send, 'outer', 0, 0))  9.54 us
    pallas_call x1, Pallas kernels, on_device(): call(descend_kernel, jax.ShapeDtypeStruct((ROWS, N), F32), [VMEM] * 9, 'd...  2.74 us
    pallas_call x1, Pallas kernels, on_device(): call(inverse_kernel, kept(LEVELS + 1, N, N), [VMEM] * 3, 'inverse')  1.81 us
    pallas_call x1, Pallas kernels, on_device(): call(leaf_kernel, (kept(N, N), kept(N_NEAR, 2 * PIECE, N)), [SMEM] + [PLA...  1.63 us
  transfers between devices with their start and end apart: 1, of which 1 were waited for; matrix products, arithmetic and copies ran while one was open for 0% of the time, Pallas kernels for 4%

profile of v6, /device:TPU:8, one launch (start us, length us, event | category | flops | bytes accessed | tf_op | source)
XLA Modules:
  0.0 78.4 jit_solution(17731708756237943367)
XLA Ops:
  0.0 1.6 %leaf.1 = (f32[128,128]{1,0:T(8,128)S(1)}, f32[16,16,128]{2,1,0:T(8,128)S(1)}) custom-call(s32[1]{0:T(128)} %bitcast.after_ref.place_ref, f32[256,128]{1,0:T(8,128)} %q_ref.1, f32[256,128]{1,0:T(8,128)} %g_ref.1, bf16[5,128,128]{2,1,0:T(8,128)(2,1)} %blocks_ref.7), custom_call_target="tpu_custom_call" | custom-call | tf_op jit(solution)/shard_map/leaf/pallas_call | solution.py:312
  1.6 0.0 copy-start
  1.6 23.3 %all_to_all.20.recv_ref = f32[16,16,128]{2,1,0:T(8,128)S(1)} all-to-all(f32[16,16,128]{2,1,0:T(8,128)S(1)} %get-tuple-element.15), channel_id=1, replica_groups=mesh['outer'=8,'far'=8,'near'=16] {'near'}, dimensions={0} | all-to-all | bytes 262144 | tf_op jit(solution)/shard_map/all_to_all | solution.py:319
  25.0 0.0 copy-done
  25.0 0.0 copy-start.1
  25.0 0.9 %near.1 = (f32[5,8,128]{2,1,0:T(8,128)S(1)}, f32[8,8,128]{2,1,0:T(8,128)}) custom-call(s32[1]{0:T(128)} %bitcast.after_ref.place_ref, f32[16,16,128]{2,1,0:T(8,128)S(1)} %all_to_all.20.recv_ref, bf16[5,128,128]{2,1,0:T(8,128)(2,1)S(1)} %copy-done), custom_call_target="tpu_custom_call" | custom-call | tf_op jit(solution)/shard_map/near/pallas_call | solution.py:320
  25.9 0.0 copy-start.4
  25.9 11.6 %all-to-all-start.1 = ((f32[8,8,128]{2,1,0:T(8,128)}), f32[8,8,128]{2,1,0:T(8,128)S(1)}, u32[]{:S(2)}, u32[]{:S(2)}) async-start(f32[8,8,128]{2,1,0:T(8,128)} %get-tuple-element.16), calls=%async_computation.1 | async-start | bytes 65536 | tf_op jit(solution)/shard_map/all_to_all | solution.py:325
  37.5 0.0 copy-done.1
  37.5 0.0 copy-done.4
  37.5 0.0 copy-start.2
  37.5 0.0 copy-start.5
  37.5 1.8 %inverse.1.inverse_ref = f32[6,128,128]{2,1,0:T(8,128)S(1)} custom-call(f32[128,128]{1,0:T(8,128)S(1)} %copy-done.4, bf16[5,128,128]{2,1,0:T(8,128)(2,1)S(1)} %copy-done.1, f32[5,8,128]{2,1,0:T(8,128)S(1)} %get-tuple-element.17.after_ref.sums_ref), custom_call_target="tpu_custom_call" | custom-call | tf_op jit(solution)/shard_map/inverse/pallas_call | solution.py:326
  39.3 0.0 copy-done.2
  39.3 0.0 copy-done.5
  39.3 1.5 %chain.1 = (f32[5,128,128]{2,1,0:T(8,128)S(1)}, f32[5,128,128]{2,1,0:T(8,128)S(1)}, f32[256,128]{1,0:T(8,128)S(1)}, f32[128,128]{1,0:T(8,128)S(1)}) custom-call(f32[128,128]{1,0:T(8,128)S(1)} %copy-done.4, f32[256,128]{1,0:T(8,128)S(1)} %copy-done.2, bf16[5,128,128]{2,1,0:T(8,128)(2,1)S(1)} %copy-done, bf16[5,128,128]{2,1,0:T(8,128)(2,1)S(1)} %copy-done.1, ...), custom_call_target="tpu_custom_call" | custom-call | tf_op jit(solution)/shard_map/chain/pallas_call | solution.py:327
  40.8 9.6 %all-to-all-done.1.recv_ref = f32[8,8,128]{2,1,0:T(8,128)S(1)} async-done(((f32[8,8,128]{2,1,0:T(8,128)}), f32[8,8,128]{2,1,0:T(8,128)S(1)}, u32[]{:S(2)}, u32[]{:S(2)}) %all-to-all-start.1) | async-done | bytes 32800 | tf_op jit(solution)/shard_map/all_to_all | solution.py:325
  50.5 0.3 far.1
  50.7 9.5 %all_to_all.21.recv_ref = f32[8,8,128]{2,1,0:T(8,128)S(1)} all-to-all(f32[8,8,128]{2,1,0:T(8,128)S(1)} %get-tuple-element.19), channel_id=1, replica_groups=mesh['outer'=8,'far'=8,'near'=16] {'outer'}, dimensions={0} | all-to-all | bytes 65536 | tf_op jit(solution)/shard_map/all_to_all | solution.py:336
  60.3 0.0 copy-start.3
  60.3 15.4 %all_to_all.22.recv_ref = f32[16,40,128]{2,1,0:T(8,128)S(1)} all-to-all(f32[16,40,128]{2,1,0:T(8,128)S(1)} %join.1), channel_id=1, replica_groups=mesh['outer'=8,'far'=8,'near'=16] {'near'}, dimensions={0} | all-to-all | bytes 655360 | tf_op jit(solution)/shard_map/all_to_all | solution.py:339
  75.7 0.0 copy-done.3
  75.7 2.7 %descend.1 = f32[256,128]{1,0:T(8,128)} custom-call(f32[16,40,128]{2,1,0:T(8,128)S(1)} %all_to_all.22.recv_ref, f32[128,128]{1,0:T(8,128)S(1)} %get-tuple-element.21.sums_ref, f32[256,128]{1,0:T(8,128)S(1)} %copy-done.3, bf16[5,128,128]{2,1,0:T(8,128)(2,1)S(1)} %copy-done, f32[5,128,128]{2,1,0:T(8,128)S(1)} %get-tuple-element.22.link_ref, ...), custom_call_target="tpu_custom_call" | custom-call | tf_op jit(solution)/shard_map/descend/pallas_call | solution.py:340
  (1 shorter events, 0.0 us)
Async XLA Ops:
  1.6 23.3 %copy-start = (bf16[5,128,128]{2,1,0:T(8,128)(2,1)S(1)}, bf16[5,128,128]{2,1,0:T(8,128)(2,1)}, u32[]{:S(2)}) copy-start(bf16[5,128,128]{2,1,0:T(8,128)(2,1)} %blocks_ref.7) | copy-start | bytes 491524
  25.0 12.5 %copy-start.1 = (bf16[5,128,128]{2,1,0:T(8,128)(2,1)S(1)}, bf16[5,128,128]{2,1,0:T(8,128)(2,1)}, u32[]{:S(2)}) copy-start(bf16[5,128,128]{2,1,0:T(8,128)(2,1)} %tris_ref.3) | copy-start | bytes 491524
  25.9 11.6 %copy-start.4 = (f32[128,128]{1,0:T(8,128)S(1)}, f32[128,128]{1,0:T(8,128)}, u32[]{:S(2)}) copy-start(f32[128,128]{1,0:T(8,128)} %tri_ref.3) | copy-start | bytes 196612
  25.9 24.6 %all-to-all-start.1 = ((f32[8,8,128]{2,1,0:T(8,128)}), f32[8,8,128]{2,1,0:T(8,128)S(1)}, u32[]{:S(2)}, u32[]{:S(2)}) async-start(f32[8,8,128]{2,1,0:T(8,128)} %get-tuple-element.16), calls=%async_computation.1 | async-start | bytes 65536 | tf_op jit(solution)/shard_map/all_to_all | solution.py:325
  37.5 1.8 %copy-start.2 = (f32[256,128]{1,0:T(8,128)S(1)}, f32[256,128]{1,0:T(8,128)}, u32[]{:S(2)}) copy-start(f32[256,128]{1,0:T(8,128)} %g_ref.1) | copy-start | bytes 393220
  37.5 1.8 %copy-start.5 = (f32[128,128]{1,0:T(8,128)S(1)}, f32[128,128]{1,0:T(8,128)}, u32[]{:S(2)}) copy-start(f32[128,128]{1,0:T(8,128)} %root_ref.1) | copy-start | bytes 196612
  60.3 15.4 %copy-start.3 = (f32[256,128]{1,0:T(8,128)S(1)}, f32[256,128]{1,0:T(8,128)}, u32[]{:S(2)}) copy-start(f32[256,128]{1,0:T(8,128)} %q_ref.1) | copy-start | bytes 393220

commit v7 on v6

--- a/solution.py
+++ b/solution.py
@@ -191,7 +191,7 @@
         send_ref[peer] = jnp.where(place // 4 == peer // 4, third, fourth)
 
 
-def far_kernel(place_ref, recv_ref, blocks_ref, after_ref, kept_ref, send_ref):
+def far_kernel(place_ref, recv_ref, blocks_ref, kept_ref, send_ref):
     place = place_ref[0]
     zero = jnp.zeros((PIECE, N), F32)
     third, fourth = zero, zero
@@ -323,20 +323,20 @@
     low = near(low)
 
     recv = near(lax.all_to_all(send, "far", 0, 0))
-    inverses = near(call(inverse_kernel, kept(LEVELS + 1, N, N), [VMEM] * 3, "inverse")(tri, tris, low))
+    high, send = call(
+        far_kernel, (kept(2, PIECE, N), kept(N_OUTER, PIECE, N)), [SMEM] + [VMEM] * 2, "far"
+    )(place, recv, blocks)
+    high = near(high)
+
+    recv = near(lax.all_to_all(send, "outer", 0, 0))
+    send = call(join_kernel, kept(N_NEAR, 5 * PIECE, N), [VMEM] * 3, "join")(recv, low, high)
+
+    recv = near(lax.all_to_all(send, "near", 0, 0))
+    inverses = near(call(inverse_kernel, kept(LEVELS + 1, N, N), [VMEM] * 3, "inverse")(tri, tris, high))
     link, gain, base, top = call(
         chain_kernel, (kept(LEVELS, N, N), kept(LEVELS, N, N), kept(ROWS, N), kept(N, N)), [VMEM] * 6, "chain"
     )(tri, cot, blocks, tris, root, inverses)
     link, gain, base, top = near(link), near(gain), near(base), near(top)
-    high, send = call(
-        far_kernel, (kept(2, PIECE, N), kept(N_OUTER, PIECE, N)), [SMEM] + [VMEM] * 3, "far"
-    )(place, recv, blocks, top)
-    high = near(high)
-
-    recv = near(lax.all_to_all(send, "outer", 0, 0))
-    send = call(join_kernel, kept(N_NEAR, 5 * PIECE, N), [VMEM] * 3, "join")(recv, low, high)
-
-    recv = near(lax.all_to_all(send, "near", 0, 0))
     return call(descend_kernel, jax.ShapeDtypeStruct((ROWS, N), F32), [VMEM] * 9, "descend")(
         recv, sums, rows, blocks, link, gain, inverses, base, top
     )

time: 78.7 us -> 79.2 us (level)
  blocking collectives: 48.2 us -> 57.1 us
  starting transfers between devices: 11.6 us -> 4.5 us
  waiting for transfers between devices: 9.61 us -> 8.18 us
    all_to_all x0 -> x1, blocking collectives: none -> 24.3 us  [on_device(): recv = near(lax.all_to_all(send, 'far', 0, 0))]
    all_to_all x2 -> x1, blocking collectives: 38.7 us -> 23.3 us  [on_device(): recv = near(lax.all_to_all(send, 'near', 0, 0))]
    all_to_all x1, starting transfers between devices: 11.6 us -> 4.5 us  [on_device(): recv = near(lax.all_to_all(send, 'near', 0, 0))]
    all_to_all x1, waiting for transfers between devices: 9.61 us -> 8.18 us  [on_device(): recv = near(lax.all_to_all(send, 'near', 0, 0))]
where the time goes in v7:
time: 79.2 us; the launch traced here: 78.8 us
  blocking collectives  57.1 us (72%)
  Pallas kernels  8.93 us (11%)
  waiting for transfers between devices  8.18 us (10%)
  starting transfers between devices  4.5 us (6%)
    all_to_all x1, blocking collectives, on_device(): recv = near(lax.all_to_all(send, 'far', 0, 0))  24.3 us
    all_to_all x1, blocking collectives, on_device(): recv = near(lax.all_to_all(send, 'near', 0, 0))  23.3 us
    all_to_all x1, blocking collectives, on_device(): recv = near(lax.all_to_all(send, 'outer', 0, 0))  9.54 us
    all_to_all x1, waiting for transfers between devices, on_device(): recv = near(lax.all_to_all(send, 'near', 0, 0))  8.18 us
    all_to_all x1, starting transfers between devices, on_device(): recv = near(lax.all_to_all(send, 'near', 0, 0))  4.5 us
    pallas_call x1, Pallas kernels, on_device(): call(descend_kernel, jax.ShapeDtypeStruct((ROWS, N), F32), [VMEM] * 9, 'd...  2.72 us
    pallas_call x1, Pallas kernels, on_device(): call(inverse_kernel, kept(LEVELS + 1, N, N), [VMEM] * 3, 'inverse')  1.81 us
    pallas_call x1, Pallas kernels, on_device(): call(leaf_kernel, (kept(N, N), kept(N_NEAR, 2 * PIECE, N)), [SMEM] + [PLA...  1.63 us
  transfers between devices with their start and end apart: 1, of which 1 were waited for; matrix products, arithmetic and copies ran while one was open for 0% of the time, Pallas kernels for 4%

profile of v7, /device:TPU:8, one launch (start us, length us, event | category | flops | bytes accessed | tf_op | source)
XLA Modules:
  0.0 78.8 jit_solution(10360064382333286059)
XLA Ops:
  0.0 1.6 %leaf.1 = (f32[128,128]{1,0:T(8,128)S(1)}, f32[16,16,128]{2,1,0:T(8,128)S(1)}) custom-call(s32[1]{0:T(128)} %bitcast.after_ref.place_ref, f32[256,128]{1,0:T(8,128)} %q_ref.1, f32[256,128]{1,0:T(8,128)} %g_ref.1, bf16[5,128,128]{2,1,0:T(8,128)(2,1)} %blocks_ref.7), custom_call_target="tpu_custom_call" | custom-call | tf_op jit(solution)/shard_map/leaf/pallas_call | solution.py:312
  1.6 0.0 copy-start
  1.6 23.3 %all_to_all.20.recv_ref = f32[16,16,128]{2,1,0:T(8,128)S(1)} all-to-all(f32[16,16,128]{2,1,0:T(8,128)S(1)} %get-tuple-element.15), channel_id=1, replica_groups=mesh['outer'=8,'far'=8,'near'=16] {'near'}, dimensions={0} | all-to-all | bytes 262144 | tf_op jit(solution)/shard_map/all_to_all | solution.py:319
  25.0 0.0 copy-done
  25.0 0.3 near.1
  25.2 24.3 %all_to_all.21.recv_ref = f32[8,8,128]{2,1,0:T(8,128)S(1)} all-to-all(f32[8,8,128]{2,1,0:T(8,128)S(1)} %get-tuple-element.16), channel_id=1, replica_groups=mesh['outer'=8,'far'=8,'near'=16] {'far'}, dimensions={0} | all-to-all | bytes 65536 | tf_op jit(solution)/shard_map/all_to_all | solution.py:325
  49.5 0.3 far.1
  49.7 9.5 %all_to_all.22.recv_ref = f32[8,8,128]{2,1,0:T(8,128)S(1)} all-to-all(f32[8,8,128]{2,1,0:T(8,128)S(1)} %get-tuple-element.17), channel_id=1, replica_groups=mesh['outer'=8,'far'=8,'near'=16] {'outer'}, dimensions={0} | all-to-all | bytes 65536 | tf_op jit(solution)/shard_map/all_to_all | solution.py:331
  59.3 0.8 join.1
  60.0 0.0 copy-start.1
  60.0 0.0 copy-start.4
  60.0 4.5 %all-to-all-start.3 = ((f32[16,40,128]{2,1,0:T(8,128)}), f32[16,40,128]{2,1,0:T(8,128)S(1)}, u32[]{:S(2)}, u32[]{:S(2)}) async-start(f32[16,40,128]{2,1,0:T(8,128)} %join.1), calls=%async_computation.3 | async-start | bytes 655360 | tf_op jit(solution)/shard_map/all_to_all | solution.py:334
  64.5 0.0 copy-done.1
  64.6 0.0 copy-done.4
  64.6 0.0 copy-start.2
  64.6 0.0 copy-start.5
  64.6 1.8 %inverse.1.inverse_ref = f32[6,128,128]{2,1,0:T(8,128)S(1)} custom-call(f32[128,128]{1,0:T(8,128)S(1)} %copy-done.4, bf16[5,128,128]{2,1,0:T(8,128)(2,1)S(1)} %copy-done.1, f32[2,8,128]{2,1,0:T(8,128)S(1)} %get-tuple-element.19.kept_ref.after_ref), custom_call_target="tpu_custom_call" | custom-call | tf_op jit(solution)/shard_map/inverse/pallas_call | solution.py:335
  66.4 0.0 copy-done.2
  66.4 0.0 copy-done.5
  66.4 0.0 copy-start.3
  66.4 1.5 %chain.1 = (f32[5,128,128]{2,1,0:T(8,128)S(1)}, f32[5,128,128]{2,1,0:T(8,128)S(1)}, f32[256,128]{1,0:T(8,128)S(1)}, f32[128,128]{1,0:T(8,128)S(1)}) custom-call(f32[128,128]{1,0:T(8,128)S(1)} %copy-done.4, f32[256,128]{1,0:T(8,128)S(1)} %copy-done.2, bf16[5,128,128]{2,1,0:T(8,128)(2,1)S(1)} %copy-done, bf16[5,128,128]{2,1,0:T(8,128)(2,1)S(1)} %copy-done.1, ...), custom_call_target="tpu_custom_call" | custom-call | tf_op jit(solution)/shard_map/chain/pallas_call | solution.py:336
  67.9 8.2 %all-to-all-done.3.recv_ref = f32[16,40,128]{2,1,0:T(8,128)S(1)} async-done(((f32[16,40,128]{2,1,0:T(8,128)}), f32[16,40,128]{2,1,0:T(8,128)S(1)}, u32[]{:S(2)}, u32[]{:S(2)}) %all-to-all-start.3) | async-done | bytes 327712 | tf_op jit(solution)/shard_map/all_to_all | solution.py:334
  76.1 0.0 copy-done.3
  76.1 2.7 %descend.1 = f32[256,128]{1,0:T(8,128)} custom-call(f32[16,40,128]{2,1,0:T(8,128)S(1)} %all-to-all-done.3.recv_ref, f32[128,128]{1,0:T(8,128)S(1)} %get-tuple-element.20.sums_ref, f32[256,128]{1,0:T(8,128)S(1)} %copy-done.3, bf16[5,128,128]{2,1,0:T(8,128)(2,1)S(1)} %copy-done, f32[5,128,128]{2,1,0:T(8,128)S(1)} %get-tuple-element.21.link_ref, ...), custom_call_target="tpu_custom_call" | custom-call | tf_op jit(solution)/shard_map/descend/pallas_call | solution.py:340
Async XLA Ops:
  1.6 23.3 %copy-start = (bf16[5,128,128]{2,1,0:T(8,128)(2,1)S(1)}, bf16[5,128,128]{2,1,0:T(8,128)(2,1)}, u32[]{:S(2)}) copy-start(bf16[5,128,128]{2,1,0:T(8,128)(2,1)} %blocks_ref.7) | copy-start | bytes 491524
  60.0 4.5 %copy-start.1 = (bf16[5,128,128]{2,1,0:T(8,128)(2,1)S(1)}, bf16[5,128,128]{2,1,0:T(8,128)(2,1)}, u32[]{:S(2)}) copy-start(bf16[5,128,128]{2,1,0:T(8,128)(2,1)} %tris_ref.3) | copy-start | bytes 491524
  60.0 4.5 %copy-start.4 = (f32[128,128]{1,0:T(8,128)S(1)}, f32[128,128]{1,0:T(8,128)}, u32[]{:S(2)}) copy-start(f32[128,128]{1,0:T(8,128)} %tri_ref.3) | copy-start | bytes 196612
  60.0 16.1 %all-to-all-start.3 = ((f32[16,40,128]{2,1,0:T(8,128)}), f32[16,40,128]{2,1,0:T(8,128)S(1)}, u32[]{:S(2)}, u32[]{:S(2)}) async-start(f32[16,40,128]{2,1,0:T(8,128)} %join.1), calls=%async_computation.3 | async-start | bytes 655360 | tf_op jit(solution)/shard_map/all_to_all | solution.py:334
  64.6 1.8 %copy-start.2 = (f32[256,128]{1,0:T(8,128)S(1)}, f32[256,128]{1,0:T(8,128)}, u32[]{:S(2)}) copy-start(f32[256,128]{1,0:T(8,128)} %g_ref.1) | copy-start | bytes 393220
  64.6 1.8 %copy-start.5 = (f32[128,128]{1,0:T(8,128)S(1)}, f32[128,128]{1,0:T(8,128)}, u32[]{:S(2)}) copy-start(f32[128,128]{1,0:T(8,128)} %root_ref.1) | copy-start | bytes 196612
  66.4 9.7 %copy-start.3 = (f32[256,128]{1,0:T(8,128)S(1)}, f32[256,128]{1,0:T(8,128)}, u32[]{:S(2)}) copy-start(f32[256,128]{1,0:T(8,128)} %q_ref.1) | copy-start | bytes 393220
